TPU v7x, 32 devices: a whole 2x2x4 slice. The times are simulated.
32 devices in a mesh: slides: 2 (over y), rows: 8 (over z, x), cols: 2 (over core).
Axes of the slice: x: 2, y: 2, z: 4, core: 2. Of those that a mesh axis runs over, the one named last changes fastest.
Arguments:
- tokens: bfloat16 [512, 32, 512], P(('slides', 'cols'), 'rows'), parts along dimension 0, may hold values from -6 to 6
- norm_gain: float32 [512], replicated, may hold values from 0.5 to 1.5
- w_in: bfloat16 [512, 2048], replicated, may hold values from -0.25 to 0.25
- w_bc: bfloat16 [512, 64], replicated, may hold values from -0.046875 to 0.046875
- rate_row: float32 [16, 1024], replicated, may hold values from 0.002 to 0.08
- rate_col: float32 [16, 1024], replicated, may hold values from 0.002 to 0.08
- skip_gain: float32 [1024], replicated, may hold values from 0.5 to 1.5
- w_out: bfloat16 [1024, 512], replicated, may hold values from -0.1875 to 0.1875
Outputs:
- mixed: bfloat16 [512, 32, 512], P(('slides', 'cols'), 'rows'), parts along dimension 0
There are 2 independent parts, one for each index of `slides`. A program takes and returns all parts, laid end to end along the dimension named above; an argument that names none is the same for every part. Nothing has to cross between parts.
All inputs are finite; a program needn't handle non-finite values.
Results may differ from a plain program's by a relative error of at most 0.013.
Values may be sent and summed in bfloat16 or wider, within the bound.
A program may use at most 64 MiB of HBM per device.

v0:
```python
import functools

import jax
import jax.numpy as jnp
from jax import lax
from jax.experimental import pallas as pl
from jax.experimental.pallas import tpu as pltpu
from jax.sharding import PartitionSpec as P

LANES = 128
VMEM_LIMIT = 60 * 1024 * 1024
MESH = pl.DeviceIdType.MESH


def normalise(tokens, gain):
    as_float = tokens.astype(jnp.float32)
    scale_now = lax.rsqrt(jnp.mean(as_float * as_float, axis=-1, keepdims=True) + 1e-05)
    return (as_float * scale_now * gain).astype(jnp.bfloat16)


def transposed_dot(a, b):
    return lax.dot_general(a, b, (((1,), (1,)), ((), ())), preferred_element_type=jnp.float32)


def spread_channels(ref, value, tiles):
    rows = value.shape[0]
    for t in range(tiles):
        ref[pl.ds(t, rows, stride=tiles), :] = value[:, t * LANES : (t + 1) * LANES]


def spread_vectors(ref, value, first, states, base):
    rows = value.shape[0]
    for n in range(states):
        ref[n, pl.ds(base, rows), :] = jnp.broadcast_to(
            value[:, first + n : first + n + 1], (rows, LANES)
        )


def scan_step(carried, decay, value, inject_ref, readout_ref, patch, start, tiles):
    new = []
    totals = [start, None]
    for n, state in enumerate(carried):
        inject = inject_ref[n, pl.ds(patch, tiles, stride=0), :]
        readout = readout_ref[n, pl.ds(patch, tiles, stride=0), :]
        state = decay[n] * state + inject * value
        term = readout * state
        totals[n % 2] = term if totals[n % 2] is None else totals[n % 2] + term
        new.append(state)
    return tuple(new), totals[0] + totals[1]


def layer_kernel(
    states, rows_n, cols_n, share, per_core,
    tok_ref, gain_in, win_in, wbc_in, rrate_in, crate_in, skip_in, wout_in,
    out_ref,
    gain_ref, win_ref, wbc_ref, rrate_ref, crate_ref, skip_ref, wout_ref, tcol, tin, rsend, rrecv, u_ref, rb_ref, rc_ref, cb_ref, cc_ref, z_ref, y_ref, gated_ref,
    rdecay, cdecay, skip_tile, stage, land, state_ref,
    tsend_sem, tin_sem, csend_sem, crecv_sem, rsend_sem, rrecv_sem, osend_sem, orecv_sem, fetch_sem,
):
    group_n = rows_n * cols_n
    pieces = tok_ref.shape[0] // share
    chunks = tin.shape[0]
    columns, width = tok_ref.shape[1:]
    inner = wout_ref.shape[0]
    tiles = inner // LANES
    piece_len = share * per_core
    chunk_len = group_n * piece_len
    blocks = stage.shape[0]
    blocks_home = blocks // cols_n
    block_len = stage.shape[1]
    r, c = lax.axis_index("rows"), lax.axis_index("cols")
    me = r * cols_n + c

    def spot(g):
        return {"rows": g // cols_n, "cols": g % cols_n}

    barrier = pltpu.get_barrier_semaphore()

    def greet(g, _):
        @pl.when(g != me)
        def _():
            pl.semaphore_signal(barrier, inc=1, device_id=spot(g), device_id_type=MESH)
        return 0

    lax.fori_loop(0, group_n, greet, 0)
    fetches = [
        pltpu.make_async_copy(src, dst, fetch_sem.at[k])
        for k, (src, dst) in enumerate((
            (rrate_in, rrate_ref), (crate_in, crate_ref), (skip_in, skip_ref), (gain_in, gain_ref),
            (wbc_in, wbc_ref), (tok_ref, tcol.at[c]), (win_in, win_ref), (wout_in, wout_ref),
        ))
    ]
    for fetch in fetches:
        fetch.start()
    pl.semaphore_wait(barrier, group_n - 1)

    local_chunks = max(1, chunks // cols_n)
    per_chunk = pieces // local_chunks

    def piece_of(k):
        piece = k // per_chunk * per_chunk + (k % per_chunk + me) % per_chunk
        place = c * pieces + piece
        return piece, place // group_n, place % group_n

    def token_copy(k):
        piece, q, g = piece_of(k)
        return g, pltpu.make_async_remote_copy(
            src_ref=tok_ref.at[pl.ds(piece * share, share)], dst_ref=tin.at[q, r],
            send_sem=tsend_sem.at[piece], recv_sem=tin_sem.at[q],
            device_id=spot(g), device_id_type=MESH,
        )

    def send_tokens(k, _):
        piece, q, g = piece_of(k)

        @pl.when(g == me)
        def _():
            pltpu.make_async_copy(tok_ref.at[pl.ds(piece * share, share)], tin.at[q, r], tin_sem.at[q]).start()

        @pl.when(g != me)
        def _():
            token_copy(k)[1].start()
        return 0

    lax.fori_loop(0, pieces, send_tokens, 0)

    def column_copy(step):
        other = (c + step) % cols_n
        return pltpu.make_async_remote_copy(
            src_ref=tok_ref, dst_ref=tcol.at[c],
            send_sem=csend_sem.at[step], recv_sem=crecv_sem.at[step],
            device_id={"cols": other}, device_id_type=MESH,
        )

    for step in range(1, cols_n):
        column_copy(step).start()

    def gate_part(tokens, core):
        tokens = tokens.astype(jnp.float32)
        own = tokens[:, :per_core]
        for k in range(1, cols_n):
            own = jnp.where(c == k, tokens[:, k * per_core : (k + 1) * per_core], own)
        normed = normalise(own.reshape(-1, width), gain_ref[...])
        count = normed.shape[0]
        base = pl.multiple_of(core * count, count)
        mixers = transposed_dot(normed, wbc_ref[...])
        mixers = mixers.astype(jnp.bfloat16).astype(jnp.float32)
        spread_vectors(cb_ref, mixers, 2 * states, states, base)
        spread_vectors(cc_ref, mixers, 3 * states, states, base)
        for k in range(0, inner, 2 * LANES):
            z_ref[pl.ds(base, count), k : k + 2 * LANES] = jnp.dot(
                normed, win_ref[:, inner + k : inner + k + 2 * LANES],
                preferred_element_type=jnp.float32,
            ).astype(jnp.bfloat16)

    for fetch in fetches:
        fetch.wait()
    spread_channels(rdecay, jnp.exp(-rrate_ref[...]), tiles)
    spread_channels(cdecay, jnp.exp(-crate_ref[...]), tiles)
    spread_channels(skip_tile, skip_ref[...], tiles)
    gate_part(tcol[c], c)

    zero = jnp.zeros((tiles, LANES), jnp.float32)
    lanes = 2 if share % 2 == 0 else 1

    def result_copy(q, k):
        g = (me + k) % group_n
        return pltpu.make_async_remote_copy(
            src_ref=rsend.at[q, pl.ds(g * piece_len, piece_len)],
            dst_ref=rrecv.at[q, pl.ds(me * piece_len, piece_len)],
            send_sem=rsend_sem.at[q, k], recv_sem=rrecv_sem.at[q],
            device_id=spot(g), device_id_type=MESH,
        )

    def row_chunk(q, _):
        pltpu.make_async_copy(tin.at[q], tin.at[q], tin_sem.at[q]).wait()
        normed = normalise(tin[q].astype(jnp.float32).reshape(chunk_len, width), gain_ref[...])
        mixers = transposed_dot(normed, wbc_ref[...])
        mixers = mixers.astype(jnp.bfloat16).astype(jnp.float32)
        spread_vectors(rb_ref, mixers, 0, states, 0)
        spread_vectors(rc_ref, mixers, states, states, 0)
        for k in range(0, tiles, 2):
            part = jnp.dot(normed, win_ref[:, k * LANES : (k + 2) * LANES],
                           preferred_element_type=jnp.float32)
            part = part.astype(jnp.bfloat16).astype(jnp.float32)
            for h in range(2):
                u_ref[pl.ds(k + h, chunk_len, stride=tiles), :] = part[:, h * LANES : (h + 1) * LANES]
        decay = [rdecay[n * tiles : (n + 1) * tiles, :] for n in range(states)]
        skip = skip_tile[...]

        def one_group(first, _):
            def one_step(j, carry):
                carry = list(carry)
                for w in range(columns):
                    for b in range(lanes):
                        row = first * lanes + b
                        patch = (j * share + row) * columns + w
                        owner = j * cols_n + w // per_core
                        value = u_ref[pl.ds(pl.multiple_of(patch * tiles, tiles), tiles), :]
                        carry[b], total = scan_step(carry[b], decay, value, rb_ref, rc_ref,
                                                    patch, skip * value, tiles)
                        rsend[q, (owner * share + row) * per_core + w % per_core] = total.astype(jnp.bfloat16)
                return tuple(carry)

            lax.fori_loop(0, rows_n, one_step, tuple((zero,) * states for _ in range(lanes)))
            return 0

        lax.fori_loop(0, share // lanes, one_group, 0)

        def send_result(k, _):
            result_copy(q, k).start()
            return 0

        pltpu.make_async_copy(
            rsend.at[q, pl.ds(me * piece_len, piece_len)],
            rrecv.at[q, pl.ds(me * piece_len, piece_len)], rrecv_sem.at[q],
        ).start()
        lax.fori_loop(1, group_n, send_result, 0)
        return 0

    lax.fori_loop(0, chunks, row_chunk, 0)

    for step in range(1, cols_n):
        column_copy(step).wait_recv()
        source = (c + cols_n - step) % cols_n
        gate_part(tcol[source], source)

    for g in range(per_core):
        for n in range(states):
            state_ref[g, n] = zero

    def out_copy(o):
        return pltpu.make_async_remote_copy(
            src_ref=stage.at[o], dst_ref=land.at[c, o % blocks_home],
            send_sem=osend_sem.at[o], recv_sem=orecv_sem.at[c, o % blocks_home],
            device_id={"cols": o // blocks_home}, device_id_type=MESH,
        )

    def col_chunk(q, _):
        pltpu.make_async_copy(rrecv.at[q], rrecv.at[q], rrecv_sem.at[q]).wait()
        decay = [cdecay[n * tiles : (n + 1) * tiles, :] for n in range(states)]
        base = q * chunk_len

        def one_step(s, carry):
            result = []
            for g in range(per_core):
                patch = s * per_core + g
                value = rrecv[q, patch].astype(jnp.float32)
                state, total = scan_step(carry[g], decay, value, cb_ref, cc_ref,
                                         base + patch, value, tiles)
                y_ref[pl.ds(pl.multiple_of(patch * tiles, tiles), tiles), :] = total
                result.append(state)
            return tuple(result)

        carry = tuple(tuple(state_ref[g, n] for n in range(states)) for g in range(per_core))
        carry = lax.fori_loop(0, chunk_len // per_core, one_step, carry)
        for g in range(per_core):
            for n in range(states):
                state_ref[g, n] = carry[g][n]
        start = pl.multiple_of(base, chunk_len)
        for t in range(tiles):
            gate = z_ref[pl.ds(start, chunk_len), t * LANES : (t + 1) * LANES].astype(jnp.float32)
            mixed = y_ref[pl.ds(t, chunk_len, stride=tiles), :]
            gated_ref[:, t * LANES : (t + 1) * LANES] = (
                mixed * (gate / (1.0 + jnp.exp(-gate)))
            ).astype(jnp.bfloat16)
        result = jnp.dot(gated_ref[...], wout_ref[...], preferred_element_type=jnp.float32)
        result = result.astype(jnp.bfloat16)
        for k in range(blocks // chunks):
            o = q * (blocks // chunks) + k
            block = result[k * block_len : (k + 1) * block_len]
            stage[o] = block

            @pl.when(o // blocks_home == c)
            def _():
                land[c, o % blocks_home] = block

            @pl.when(o // blocks_home != c)
            def _():
                out_copy(o).start()
        return 0

    lax.fori_loop(0, chunks, col_chunk, 0)

    def drain_tokens(k, _):
        g, copy = token_copy(k)

        @pl.when(g != me)
        def _():
            copy.wait_send()
        return 0

    lax.fori_loop(0, pieces, drain_tokens, 0)
    for step in range(1, cols_n):
        column_copy(step).wait_send()

    def drain_results(q, _):
        def one(k, _):
            result_copy(q, k).wait_send()
            return 0
        return lax.fori_loop(1, group_n, one, 0)

    lax.fori_loop(0, chunks, drain_results, 0)

    def drain_out(o, _):
        @pl.when(o // blocks_home != c)
        def _():
            out_copy(o).wait_send()
        return 0

    lax.fori_loop(0, blocks, drain_out, 0)
    for source in range(cols_n):
        @pl.when(source != c)
        def _():
            for i in range(blocks_home):
                pltpu.make_async_copy(
                    land.at[source, i], land.at[source, i], orecv_sem.at[source, i]
                ).wait()
    for i in range(blocks_home):
        parts = [
            land[s, i].astype(jnp.float32).reshape(block_len // per_core, per_core, -1)
            for s in range(cols_n)
        ]
        rows = block_len // per_core
        out_ref[i * rows : (i + 1) * rows] = jnp.concatenate(parts, axis=1).astype(jnp.bfloat16)


def per_device(tokens, norm_gain, w_in, w_bc, rate_row, rate_col, skip_gain, w_out):
    inner, width_out = w_out.shape
    states = rate_row.shape[0]
    height, columns, width = tokens.shape
    rows_n, cols_n = lax.axis_size("rows"), lax.axis_size("cols")
    group_n = rows_n * cols_n
    per_core = columns // cols_n
    total = height * cols_n
    share = min(4, total // group_n)
    chunks = total // (group_n * share)
    pieces = height // share
    piece_len = share * per_core
    chunk_len = group_n * piece_len
    tiles = inner // LANES
    blocks = max(chunks, cols_n)
    block_len = total * per_core // blocks
    patches = total * per_core
    f32, bf16 = jnp.float32, jnp.bfloat16
    dma = pltpu.SemaphoreType.DMA
    out = pl.pallas_call(
        functools.partial(layer_kernel, states, rows_n, cols_n, share, per_core),
        in_specs=[pl.BlockSpec(memory_space=pl.ANY)] * 8,
        out_specs=pl.BlockSpec(memory_space=pltpu.VMEM),
        out_shape=jax.ShapeDtypeStruct((height, columns, width_out), bf16),
        scratch_shapes=[
            pltpu.VMEM((1, width), f32),
            pltpu.VMEM(w_in.shape, bf16),
            pltpu.VMEM(w_bc.shape[::-1], bf16),
            pltpu.VMEM(rate_row.shape, f32),
            pltpu.VMEM(rate_col.shape, f32),
            pltpu.VMEM((1, inner), f32),
            pltpu.VMEM(w_out.shape, bf16),
            pltpu.VMEM((cols_n, height, columns, width), bf16),
            pltpu.VMEM((chunks, rows_n, share, columns, width), bf16),
            pltpu.VMEM((chunks, chunk_len, tiles, LANES), bf16),
            pltpu.VMEM((chunks, chunk_len, tiles, LANES), bf16),
            pltpu.VMEM((chunk_len * tiles, LANES), f32),
            pltpu.VMEM((states, chunk_len + 8, LANES), f32),
            pltpu.VMEM((states, chunk_len + 8, LANES), f32),
            pltpu.VMEM((states, patches + 8, LANES), f32),
            pltpu.VMEM((states, patches + 8, LANES), f32),
            pltpu.VMEM((patches, inner), bf16),
            pltpu.VMEM((chunk_len * tiles, LANES), f32),
            pltpu.VMEM((chunk_len, inner), bf16),
            pltpu.VMEM((states * tiles, LANES), f32),
            pltpu.VMEM((states * tiles, LANES), f32),
            pltpu.VMEM((tiles, LANES), f32),
            pltpu.VMEM((blocks, block_len, width_out), bf16),
            pltpu.VMEM((cols_n, blocks // cols_n, block_len, width_out), bf16),
            pltpu.VMEM((per_core, states, tiles, LANES), f32),
            dma((pieces,)), dma((chunks,)), dma((cols_n,)), dma((cols_n,)),
            dma((chunks, group_n)), dma((chunks,)), dma((blocks,)),
            dma((cols_n, blocks // cols_n)), dma((8,)),
        ],
        compiler_params=pltpu.CompilerParams(
            vmem_limit_bytes=VMEM_LIMIT, collective_id=0, has_side_effects=True
        ),
        name="layer",
    )(tokens, norm_gain[None], w_in, w_bc.T, rate_row, rate_col, skip_gain[None], w_out)
    return out


def solution(mesh):
    placed = (P(("slides", "cols"), "rows", None), P(), P(), P(), P(), P(), P(), P())
    return jax.shard_map(
        per_device,
        mesh=mesh,
        in_specs=placed,
        out_specs=P(("slides", "cols"), "rows", None),
        check_vma=False,
    )
```

profile of v0, /device:TPU:0, one launch (start us, length us, event | category | flops | bytes accessed | tf_op | source)
XLA Modules:
  0.0 47.5 jit_solution(5799739382262883145)
XLA Ops:
  0.0 45.5 %layer.1 = bf16[128,4,512]{2,1,0:T(4,128)(2,1)} custom-call(bf16[128,4,512]{2,1,0:T(4,128)(2,1)} %tok_ref.1, f32[1,512]{1,0:T(1,128)} %bitcast.5, bf16[512,2048]{1,0:T(8,128)(2,1)} %win_in.1, bf16[64,512]{1,0:T(8,128)(2,1)} %bitcast.3, f32[16,1024]{1,0:T(8,128)} %rrate_in.1, f32[16,1024]{1,0:T(8,128)} %crate_in.1, f32[1,1024]{1,0:T(1,128)} %bitcast.4, ...), custom_call_target="tpu_custom_call" | custom-call | tf_op jit(solution)/shard_map/layer/pallas_call | solution.py:347
  45.5 2.0 %copy.10 = bf16[128,4,512]{2,1,0:T(4,128)(2,1)} copy(bf16[128,4,512]{2,1,0:T(4,128)(2,1)} %layer.1) | data formatting | bytes 1048576
where the time goes:
time: 47.7 us; the launch traced here: 47.5 us
  Pallas kernels  45.5 us (95%)
  local copies, waits for them, and re-layouts  2.02 us (4%)
    pallas_call x1, Pallas kernels, per_device(): pl.pallas_call(functools.partial(layer_kernel, states, rows_n, cols_n, sh...  45.5 us
    unnamed x1, local copies, waits for them, and re-layouts  2.02 us

commit v1 on v0

--- a/solution.py
+++ b/solution.py
@@ -325,7 +325,7 @@
         out_ref[i * rows : (i + 1) * rows] = jnp.concatenate(parts, axis=1).astype(jnp.bfloat16)
 
 
-def per_device(tokens, norm_gain, w_in, w_bc, rate_row, rate_col, skip_gain, w_out):
+def per_device_uniform(tokens, norm_gain, w_in, w_bc, rate_row, rate_col, skip_gain, w_out):
     inner, width_out = w_out.shape
     states = rate_row.shape[0]
     height, columns, width = tokens.shape
@@ -387,6 +387,494 @@
     return out
 
 
+LANE_PAIR = 2 * LANES
+
+
+def grouped_kernel(
+    states, rows_n, cols_n, chunks, per_core,
+    tok_ref, gain_in, win_in, wbc_in, rrate_in, crate_in, skip_in, wout_in,
+    out_ref,
+    gain_ref, win_ref, wbc_ref, rrate_ref, crate_ref, skip_ref, wout_ref,
+    tcol, tin_a, tin_b, tin_c, table, order_ref, normed_ref, u_ref, b_ref, c_ref, lag_ref, ys_ref,
+    rsend, rrecv, cb_ref, cc_ref, z_ref, y_ref, gated_ref, cdecay, stage, land, state_ref,
+    tsend_sem, own_sem, early_sem, relay_sem, csend_sem, crecv_sem, rsend_sem, rrecv_sem,
+    osend_sem, orecv_sem, fetch_sem,
+):
+    height, columns, width = tok_ref.shape
+    inner = wout_ref.shape[0]
+    tiles = inner // LANES
+    pairs = inner // LANE_PAIR
+    quarter = rows_n // 4
+    chunk_rows = height * cols_n // chunks
+    chunk_len = chunk_rows * per_core
+    local_chunks = chunks // cols_n
+    blocks = stage.shape[0]
+    blocks_home = blocks // cols_n
+    block_len = stage.shape[1]
+    r, c = lax.axis_index("rows"), lax.axis_index("cols")
+    lines = quarter * cols_n
+    long_rows = chunk_rows // lines
+    short_rows = long_rows // 2
+
+    groups = ((0, quarter, long_rows), (quarter, quarter, long_rows), (2 * quarter, 2 * quarter, short_rows))
+    inside = (r < quarter, (r >= quarter) & (r < 2 * quarter), r >= 2 * quarter)
+
+    def line_of(group, k):
+        first, chips, _ = groups[group]
+        chip, core = k // cols_n, k % cols_n
+        return (chip % quarter) * cols_n + core, chip // quarter, first + chip, core
+
+    def row_offset(group, k):
+        line, half, _, _ = line_of(group, k)
+        return line * long_rows + half * short_rows
+
+    barrier = pltpu.get_barrier_semaphore()
+
+    def greet(chip, core):
+        pl.semaphore_signal(barrier, inc=1, device_id={"rows": chip, "cols": core}, device_id_type=MESH)
+
+    for group, (first, chips, _) in enumerate(groups):
+        @pl.when(inside[group])
+        def _():
+            me = (r - first) * cols_n + c
+
+            def one(k, _):
+                @pl.when(k != me)
+                def _():
+                    greet(first + k // cols_n, k % cols_n)
+                return 0
+
+            lax.fori_loop(0, chips * cols_n, one, 0)
+            if group == 1:
+                greet(r - quarter, c)
+            if group == 2:
+                greet(quarter + (r - first) % quarter, c)
+
+    fetches = [
+        pltpu.make_async_copy(src, dst, fetch_sem.at[k])
+        for k, (src, dst) in enumerate((
+            (rrate_in, rrate_ref), (crate_in, crate_ref), (skip_in, skip_ref), (gain_in, gain_ref),
+            (wbc_in, wbc_ref), (tok_ref, tcol.at[c]), (win_in, win_ref), (wout_in, wout_ref),
+        ))
+    ]
+    for fetch in fetches:
+        fetch.start()
+
+    for group, (first, chips, _) in enumerate(groups):
+        @pl.when(inside[group])
+        def _():
+            pl.semaphore_wait(barrier, chips * cols_n - 1 + (1, 2, 0)[group])
+
+    tins = (tin_a, tin_b, tin_c)
+    early = (0, quarter, 2 * quarter)
+
+    def own_copy(group, n):
+        first, chips, rows = groups[group]
+        part, k = n // (chips * cols_n), n % (chips * cols_n)
+        me = (r - first) * cols_n + c
+        k = (k + me) % (chips * cols_n)
+        _, _, chip, core = line_of(group, k)
+        q = c * local_chunks + part
+        src = tok_ref.at[pl.ds(part * chunk_rows + row_offset(group, k), rows)]
+        dst = tins[group].at[q, early[group] + r - first]
+        remote = pltpu.make_async_remote_copy(
+            src_ref=src, dst_ref=dst, send_sem=tsend_sem.at[n], recv_sem=own_sem.at[q],
+            device_id={"rows": chip, "cols": core}, device_id_type=MESH,
+        )
+        return k != me, remote, lambda: pltpu.make_async_copy(src, dst, own_sem.at[q])
+
+    for group, (first, chips, _) in enumerate(groups):
+        @pl.when(inside[group])
+        def _():
+            def one(n, _):
+                away, remote, local = own_copy(group, n)
+
+                @pl.when(away)
+                def _():
+                    remote.start()
+
+                @pl.when(jnp.logical_not(away))
+                def _():
+                    local().start()
+                return 0
+
+            lax.fori_loop(0, local_chunks * chips * cols_n, one, 0)
+
+    def column_copy(step):
+        other = (c + step) % cols_n
+        return pltpu.make_async_remote_copy(
+            src_ref=tok_ref, dst_ref=tcol.at[c],
+            send_sem=csend_sem.at[step], recv_sem=crecv_sem.at[step],
+            device_id={"cols": other}, device_id_type=MESH,
+        )
+
+    for step in range(1, cols_n):
+        column_copy(step).start()
+
+    def gate_part(tokens, core):
+        tokens = tokens.astype(jnp.float32)
+        own = tokens[:, :per_core]
+        for k in range(1, cols_n):
+            own = jnp.where(c == k, tokens[:, k * per_core : (k + 1) * per_core], own)
+        normed = normalise(own.reshape(-1, width), gain_ref[...])
+        count = normed.shape[0]
+        base = pl.multiple_of(core * count, count)
+        mixers = transposed_dot(normed, wbc_ref[...])
+        mixers = mixers.astype(jnp.bfloat16).astype(jnp.float32)
+        spread_vectors(cb_ref, mixers, 2 * states, states, base)
+        spread_vectors(cc_ref, mixers, 3 * states, states, base)
+        for k in range(0, inner, LANE_PAIR):
+            z_ref[pl.ds(base, count), k : k + LANE_PAIR] = jnp.dot(
+                normed, win_ref[:, inner + k : inner + k + LANE_PAIR],
+                preferred_element_type=jnp.float32,
+            ).astype(jnp.bfloat16)
+
+    for fetch in fetches:
+        fetch.wait()
+
+    for group, (first, chips, _) in enumerate(groups):
+        @pl.when(inside[group])
+        def _():
+            rate = [rrate_ref[:, k * LANE_PAIR : (k + 1) * LANE_PAIR] for k in range(pairs)]
+            for k in range(pairs):
+                def fill(d, _):
+                    table[k, d] = jnp.exp(-rate[k] * d.astype(jnp.float32)).astype(jnp.bfloat16)
+                    return 0
+
+                lax.fori_loop(0, (early[group] + chips) * columns, fill, 0)
+
+    spread_channels(cdecay, jnp.exp(-crate_ref[...]), tiles)
+    zero = jnp.zeros((tiles, LANES), jnp.float32)
+    for g in range(per_core):
+        for n in range(states):
+            state_ref[g, n] = zero
+    gate_part(tcol[c], c)
+    for step in range(1, cols_n):
+        column_copy(step).wait_recv()
+        source = (c + cols_n - step) % cols_n
+        gate_part(tcol[source], source)
+
+    def relay_copy(group, q, half):
+        if group == 0:
+            src, dst = tin_a.at[q], tin_b.at[q, pl.ds(0, quarter)]
+            chip = r + quarter
+        else:
+            src = tin_b.at[q, :, pl.ds(half * short_rows, short_rows)]
+            dst = tin_c.at[q, pl.ds(0, 2 * quarter)]
+            chip = r + quarter + half * quarter
+        return pltpu.make_async_remote_copy(
+            src_ref=src, dst_ref=dst, send_sem=relay_sem.at[q, half], recv_sem=early_sem.at[q],
+            device_id={"rows": chip}, device_id_type=MESH,
+        )
+
+    def result_copy(group, q, k):
+        first, chips, rows = groups[group]
+        count = chips * cols_n
+        me = (r - first) * cols_n + c
+        g = (me + k) % count
+        patches = rows * per_core
+        src = rsend.at[q, pl.ds(g * patches, patches)]
+        dst = rrecv.at[q, pl.ds(row_offset(group, me) * per_core, patches)]
+        remote = pltpu.make_async_remote_copy(
+            src_ref=src, dst_ref=dst, send_sem=rsend_sem.at[q, k], recv_sem=rrecv_sem.at[q],
+            device_id={"rows": first + g // cols_n, "cols": g % cols_n}, device_id_type=MESH,
+        )
+        return remote, lambda: pltpu.make_async_copy(src, dst, rrecv_sem.at[q])
+
+    def row_chunk(group, q):
+        first, chips, rows = groups[group]
+        tin = tins[group]
+        before = early[group]
+        if before:
+            part = tin.at[q, pl.ds(0, before)]
+            pltpu.make_async_copy(part, part, early_sem.at[q]).wait()
+        part = tin.at[q, pl.ds(before, chips)]
+        pltpu.make_async_copy(part, part, own_sem.at[q]).wait()
+        for half in range((1, 2, 0)[group]):
+            relay_copy(group, q, half).start()
+        sources = before + chips
+        out_cols, pre_cols = chips * columns, before * columns
+        all_cols = out_cols + pre_cols
+        block = columns * rows
+        for s in range(sources):
+            arrived = tin[q, s].astype(jnp.float32).reshape(block, width)
+            for t in range(width // LANES):
+                order_ref[t, s * block : (s + 1) * block] = arrived[:, t * LANES : (t + 1) * LANES]
+        for s in range(sources):
+            ordered = jnp.concatenate([
+                jnp.concatenate(
+                    [order_ref[t, pl.ds(s * block + w, rows, stride=columns), :] for w in range(columns)], axis=0
+                )
+                for t in range(width // LANES)
+            ], axis=1)
+            normed_ref[s * block : (s + 1) * block] = normalise(ordered, gain_ref[...])
+        normed = normed_ref[: all_cols * rows]
+        b_ref[: all_cols * rows] = transposed_dot(normed, wbc_ref[:states]).astype(jnp.bfloat16).astype(jnp.float32)
+        c_ref[: out_cols * rows] = transposed_dot(
+            normed_ref[pre_cols * rows : all_cols * rows], wbc_ref[states : 2 * states]
+        ).astype(jnp.bfloat16).astype(jnp.float32)
+        for k in range(pairs):
+            u_ref[k, : all_cols * rows] = jnp.dot(
+                normed, win_ref[:, k * LANE_PAIR : (k + 1) * LANE_PAIR], preferred_element_type=jnp.float32
+            ).astype(jnp.bfloat16).astype(jnp.float32)
+
+        def span(d):
+            low = max(0, d - pre_cols)
+            return low, out_cols - low, pre_cols + low - d
+
+        for d in range(all_cols):
+            low, count, source = span(d)
+            lag_ref[d, : count * rows] = (
+                c_ref[low * rows : out_cols * rows] * b_ref[source * rows : (source + count) * rows]
+            ).astype(jnp.bfloat16)
+
+        def one_pair(k, _):
+            skip = skip_ref[k]
+            total = [
+                skip * u_ref[k, (pre_cols + o) * rows : (pre_cols + o + 1) * rows] for o in range(out_cols)
+            ]
+            for d in range(all_cols):
+                low, count, source = span(d)
+                weight = jnp.dot(lag_ref[d, : count * rows], table[k, d], preferred_element_type=jnp.float32)
+                for i in range(count):
+                    total[low + i] += weight[i * rows : (i + 1) * rows] * u_ref[
+                        k, (source + i) * rows : (source + i + 1) * rows
+                    ]
+            for o in range(out_cols):
+                for h in range(2):
+                    ys_ref[pl.ds(o * rows * tiles + 2 * k + h, rows, stride=tiles), :] = (
+                        total[o][:, h * LANES : (h + 1) * LANES]
+                    )
+            return 0
+
+        lax.fori_loop(0, pairs, one_pair, 0)
+
+        def pack(i, _):
+            for w in range(per_core):
+                for v in range(rows):
+                    at = ((i * per_core + w) * rows + v) * tiles
+                    rsend[q, (i * rows + v) * per_core + w] = (
+                        ys_ref[pl.ds(pl.multiple_of(at, tiles), tiles), :].astype(jnp.bfloat16)
+                    )
+            return 0
+
+        lax.fori_loop(0, out_cols // per_core, pack, 0)
+        result_copy(group, q, 0)[1]().start()
+
+        def send_result(k, _):
+            result_copy(group, q, k)[0].start()
+            return 0
+
+        lax.fori_loop(1, chips * cols_n, send_result, 0)
+
+    def out_copy(o):
+        return pltpu.make_async_remote_copy(
+            src_ref=stage.at[o], dst_ref=land.at[c, o % blocks_home],
+            send_sem=osend_sem.at[o], recv_sem=orecv_sem.at[c, o % blocks_home],
+            device_id={"cols": o // blocks_home}, device_id_type=MESH,
+        )
+
+    def col_chunk(q):
+        pltpu.make_async_copy(rrecv.at[q], rrecv.at[q], rrecv_sem.at[q]).wait()
+        decay = [cdecay[n * tiles : (n + 1) * tiles, :] for n in range(states)]
+        base = q * chunk_len
+
+        def one_step(s, carry):
+            result = []
+            for g in range(per_core):
+                patch = s * per_core + g
+                value = rrecv[q, patch].astype(jnp.float32)
+                state, total = scan_step(carry[g], decay, value, cb_ref, cc_ref,
+                                         base + patch, value, tiles)
+                y_ref[pl.ds(pl.multiple_of(patch * tiles, tiles), tiles), :] = total
+                result.append(state)
+            return tuple(result)
+
+        carry = tuple(tuple(state_ref[g, n] for n in range(states)) for g in range(per_core))
+        carry = lax.fori_loop(0, chunk_len // per_core, one_step, carry)
+        for g in range(per_core):
+            for n in range(states):
+                state_ref[g, n] = carry[g][n]
+        start = pl.multiple_of(base, chunk_len)
+        for t in range(tiles):
+            gate = z_ref[pl.ds(start, chunk_len), t * LANES : (t + 1) * LANES].astype(jnp.float32)
+            mixed = y_ref[pl.ds(t, chunk_len, stride=tiles), :]
+            gated_ref[:, t * LANES : (t + 1) * LANES] = (
+                mixed * (gate / (1.0 + jnp.exp(-gate)))
+            ).astype(jnp.bfloat16)
+        result = jnp.dot(gated_ref[...], wout_ref[...], preferred_element_type=jnp.float32)
+        result = result.astype(jnp.bfloat16)
+        for k in range(blocks // chunks):
+            o = q * (blocks // chunks) + k
+            block = result[k * block_len : (k + 1) * block_len]
+            stage[o] = block
+
+            @pl.when(o // blocks_home == c)
+            def _():
+                land[c, o % blocks_home] = block
+
+            @pl.when(o // blocks_home != c)
+            def _():
+                out_copy(o).start()
+
+    def one_chunk(q, _):
+        @pl.when(q < chunks)
+        def _():
+            for group in range(3):
+                @pl.when(inside[group])
+                def _():
+                    row_chunk(group, q)
+
+        @pl.when(q > 0)
+        def _():
+            col_chunk(q - 1)
+        return 0
+
+    lax.fori_loop(0, chunks + 1, one_chunk, 0)
+
+    for group, (first, chips, _) in enumerate(groups):
+        @pl.when(inside[group])
+        def _():
+            def drain_tokens(n, _):
+                away, remote, _ = own_copy(group, n)
+
+                @pl.when(away)
+                def _():
+                    remote.wait_send()
+                return 0
+
+            lax.fori_loop(0, local_chunks * chips * cols_n, drain_tokens, 0)
+
+            def drain_chunk(q, _):
+                for half in range((1, 2, 0)[group]):
+                    relay_copy(group, q, half).wait_send()
+
+                def one(k, _):
+                    result_copy(group, q, k)[0].wait_send()
+                    return 0
+                return lax.fori_loop(1, chips * cols_n, one, 0)
+
+            lax.fori_loop(0, chunks, drain_chunk, 0)
+
+    for step in range(1, cols_n):
+        column_copy(step).wait_send()
+
+    def drain_out(o, _):
+        @pl.when(o // blocks_home != c)
+        def _():
+            out_copy(o).wait_send()
+        return 0
+
+    lax.fori_loop(0, blocks, drain_out, 0)
+    for source in range(cols_n):
+        @pl.when(source != c)
+        def _():
+            for i in range(blocks_home):
+                pltpu.make_async_copy(
+                    land.at[source, i], land.at[source, i], orecv_sem.at[source, i]
+                ).wait()
+    for i in range(blocks_home):
+        parts = [
+            land[s, i].astype(jnp.float32).reshape(block_len // per_core, per_core, -1)
+            for s in range(cols_n)
+        ]
+        rows = block_len // per_core
+        out_ref[i * rows : (i + 1) * rows] = jnp.concatenate(parts, axis=1).astype(jnp.bfloat16)
+
+
+def per_device_grouped(chunks, tokens, norm_gain, w_in, w_bc, rate_row, rate_col, skip_gain, w_out):
+    inner, width_out = w_out.shape
+    states = rate_row.shape[0]
+    height, columns, width = tokens.shape
+    rows_n, cols_n = lax.axis_size("rows"), lax.axis_size("cols")
+    quarter = rows_n // 4
+    per_core = columns // cols_n
+    total = height * cols_n
+    chunk_rows = total // chunks
+    chunk_len = chunk_rows * per_core
+    long_rows = chunk_rows // (quarter * cols_n)
+    short_rows = long_rows // 2
+    tiles = inner // LANES
+    pairs = inner // LANE_PAIR
+    blocks = max(chunks, cols_n)
+    block_len = total * per_core // blocks
+    patches = total * per_core
+    lags = rows_n * columns
+    held = lags * short_rows
+    outs = 2 * quarter * columns * short_rows
+    f32, bf16 = jnp.float32, jnp.bfloat16
+    dma = pltpu.SemaphoreType.DMA
+    return pl.pallas_call(
+        functools.partial(grouped_kernel, states, rows_n, cols_n, chunks, per_core),
+        in_specs=[pl.BlockSpec(memory_space=pl.ANY)] * 8,
+        out_specs=pl.BlockSpec(memory_space=pltpu.VMEM),
+        out_shape=jax.ShapeDtypeStruct((height, columns, width_out), bf16),
+        scratch_shapes=[
+            pltpu.VMEM((1, width), f32),
+            pltpu.VMEM(w_in.shape, bf16),
+            pltpu.VMEM(w_bc.shape[::-1], bf16),
+            pltpu.VMEM(rate_row.shape, f32),
+            pltpu.VMEM(rate_col.shape, f32),
+            pltpu.VMEM((pairs, 1, LANE_PAIR), f32),
+            pltpu.VMEM(w_out.shape, bf16),
+            pltpu.VMEM((cols_n, height, columns, width), bf16),
+            pltpu.VMEM((chunks, quarter, long_rows, columns, width), bf16),
+            pltpu.VMEM((chunks, 2 * quarter, long_rows, columns, width), bf16),
+            pltpu.VMEM((chunks, 4 * quarter, short_rows, columns, width), bf16),
+            pltpu.VMEM((pairs, lags, states, LANE_PAIR), bf16),
+            pltpu.VMEM((width // LANES, held, LANES), f32),
+            pltpu.VMEM((held, width), bf16),
+            pltpu.VMEM((pairs, held, LANE_PAIR), f32),
+            pltpu.VMEM((held, states), f32),
+            pltpu.VMEM((outs, states), f32),
+            pltpu.VMEM((lags, outs, states), bf16),
+            pltpu.VMEM((outs * tiles, LANES), f32),
+            pltpu.VMEM((chunks, chunk_len, tiles, LANES), bf16),
+            pltpu.VMEM((chunks, chunk_len, tiles, LANES), bf16),
+            pltpu.VMEM((states, patches + 8, LANES), f32),
+            pltpu.VMEM((states, patches + 8, LANES), f32),
+            pltpu.VMEM((patches, inner), bf16),
+            pltpu.VMEM((chunk_len * tiles, LANES), f32),
+            pltpu.VMEM((chunk_len, inner), bf16),
+            pltpu.VMEM((states * tiles, LANES), f32),
+            pltpu.VMEM((blocks, block_len, width_out), bf16),
+            pltpu.VMEM((cols_n, blocks // cols_n, block_len, width_out), bf16),
+            pltpu.VMEM((per_core, states, tiles, LANES), f32),
+            dma((chunks // cols_n * 2 * quarter * cols_n,)), dma((chunks,)), dma((chunks,)), dma((chunks, 2)),
+            dma((cols_n,)), dma((cols_n,)),
+            dma((chunks, 2 * quarter * cols_n)), dma((chunks,)), dma((blocks,)),
+            dma((cols_n, blocks // cols_n)), dma((8,)),
+        ],
+        compiler_params=pltpu.CompilerParams(
+            vmem_limit_bytes=VMEM_LIMIT, collective_id=0, has_side_effects=True
+        ),
+        name="layer",
+    )(
+        tokens, norm_gain[None], w_in, w_bc.T, rate_row, rate_col,
+        skip_gain.reshape(pairs, 1, LANE_PAIR), w_out,
+    )
+
+
+def chunk_count(tokens, inner):
+    height, columns, _ = tokens.shape
+    rows_n, cols_n = lax.axis_size("rows"), lax.axis_size("cols")
+    total = height * cols_n
+    if rows_n % 4 or columns % cols_n or inner % LANE_PAIR:
+        return 0
+    step = rows_n // 2 * cols_n * 8
+    if total % step or total // step % cols_n:
+        return 0
+    return total // step
+
+
+def per_device(tokens, norm_gain, w_in, w_bc, rate_row, rate_col, skip_gain, w_out):
+    args = (tokens, norm_gain, w_in, w_bc, rate_row, rate_col, skip_gain, w_out)
+    chunks = chunk_count(tokens, w_out.shape[0])
+    if chunks:
+        return per_device_grouped(chunks, *args)
+    return per_device_uniform(*args)
+
+
 def solution(mesh):
     placed = (P(("slides", "cols"), "rows", None), P(), P(), P(), P(), P(), P(), P())
     return jax.shard_map(

time: 47.7 us -> 52.3 us (1.096)
  the two profiles are of different devices: /device:TPU:0 before, /device:TPU:17 now
where the time goes in v1:
time: 52.3 us; the launch traced here: 51.5 us
  Pallas kernels  49.5 us (95%)
  local copies, waits for them, and re-layouts  2.02 us (4%)
    pallas_call x1, Pallas kernels, per_device_grouped(): pl.pallas_call(functools.partial(grouped_kernel, states, rows_n, cols_n,...  49.5 us
    unnamed x1, local copies, waits for them, and re-layouts  2.02 us

profile of v1, /device:TPU:17, one launch (start us, length us, event | category | flops | bytes accessed | tf_op | source)
XLA Modules:
  0.0 51.5 jit_solution(3270130463220317078)
XLA Ops:
  0.0 49.5 %layer.1 = bf16[128,4,512]{2,1,0:T(4,128)(2,1)} custom-call(bf16[128,4,512]{2,1,0:T(4,128)(2,1)} %tok_ref.1, f32[1,512]{1,0:T(1,128)} %bitcast.5, bf16[512,2048]{1,0:T(8,128)(2,1)} %win_in.1, bf16[64,512]{1,0:T(8,128)(2,1)} %bitcast.3, f32[16,1024]{1,0:T(8,128)} %rrate_in.1, f32[16,1024]{1,0:T(8,128)} %crate_in.1, f32[4,1,256]{2,1,0:T(1,128)} %bitcast.4, ...), custom_call_target="tpu_custom_call" | custom-call | tf_op jit(solution)/shard_map/layer/pallas_call | solution.py:807
  49.5 2.0 %copy.10 = bf16[128,4,512]{2,1,0:T(4,128)(2,1)} copy(bf16[128,4,512]{2,1,0:T(4,128)(2,1)} %layer.1) | data formatting | bytes 1048576

commit v2 on v0

--- a/solution.py
+++ b/solution.py
@@ -325,7 +325,7 @@
         out_ref[i * rows : (i + 1) * rows] = jnp.concatenate(parts, axis=1).astype(jnp.bfloat16)
 
 
-def per_device(tokens, norm_gain, w_in, w_bc, rate_row, rate_col, skip_gain, w_out):
+def per_device_uniform(tokens, norm_gain, w_in, w_bc, rate_row, rate_col, skip_gain, w_out):
     inner, width_out = w_out.shape
     states = rate_row.shape[0]
     height, columns, width = tokens.shape
@@ -387,6 +387,526 @@
     return out
 
 
+LANE_PAIR = 2 * LANES
+SUBLANES = 8
+
+
+def grouped_kernel(
+    states, rows_n, cols_n, chunks, per_core,
+    tok_ref, gain_in, win_in, wbc_in, rrate_in, crate_in, skip_in, wout_in,
+    out_ref,
+    gain_ref, win_ref, wbc_ref, rrate_ref, crate_ref, skip_ref, wout_ref,
+    tcol, tin_a, tin_b, tin_c, table, order_ref, normed_ref, u_ref, b_ref, c_ref, lag_ref,
+    rsend, rrecv, vcol, inject_ref, spread_ref, read_ref, hist, z_ref, gated_ref, stage, land, state_ref,
+    own_send_sem, next_send_sem, own_sem, early_sem, relay_sem, csend_sem, crecv_sem, rsend_sem, rrecv_sem,
+    osend_sem, orecv_sem, fetch_sem,
+):
+    height, columns, width = tok_ref.shape
+    inner = wout_ref.shape[0]
+    tiles = inner // LANES
+    pairs = inner // LANE_PAIR
+    quarter = rows_n // 4
+    total = height * cols_n
+    chunk_rows = total // chunks
+    local_chunks = chunks // cols_n
+    lines = quarter * cols_n
+    rows = chunk_rows // lines
+    run = LANE_PAIR // states
+    r, c = lax.axis_index("rows"), lax.axis_index("cols")
+
+    groups = ((0, quarter), (quarter, quarter), (2 * quarter, 2 * quarter))
+    inside = (r < quarter, (r >= quarter) & (r < 2 * quarter), r >= 2 * quarter)
+    tins = (tin_a, tin_b, tin_c)
+    early = (0, quarter, 2 * quarter)
+    line = r % quarter * cols_n + c
+
+    def chip_of(group, q, p):
+        chip = groups[group][0] + p // cols_n
+        return chip + q % 2 * quarter if group == 2 else chip
+
+    def slot(group, q):
+        return q // 2 if group == 2 else q
+
+    barrier = pltpu.get_barrier_semaphore()
+
+    def greet(chip, core):
+        pl.semaphore_signal(barrier, inc=1, device_id={"rows": chip, "cols": core}, device_id_type=MESH)
+
+    for group, (first, chips) in enumerate(groups):
+        @pl.when(inside[group])
+        def _():
+            me = (r - first) * cols_n + c
+
+            def one(k, _):
+                @pl.when(k != me)
+                def _():
+                    greet(first + k // cols_n, k % cols_n)
+                return 0
+
+            lax.fori_loop(0, chips * cols_n, one, 0)
+            if group:
+                def back(k, _):
+                    greet(first - quarter + k // cols_n, k % cols_n)
+                    return 0
+
+                lax.fori_loop(0, lines, back, 0)
+
+    fetches = [
+        pltpu.make_async_copy(src, dst, fetch_sem.at[k])
+        for k, (src, dst) in enumerate((
+            (rrate_in, rrate_ref), (crate_in, crate_ref), (skip_in, skip_ref), (gain_in, gain_ref),
+            (wbc_in, wbc_ref), (tok_ref, tcol.at[c]), (win_in, win_ref), (wout_in, wout_ref),
+        ))
+    ]
+    for fetch in fetches:
+        fetch.start()
+
+    for group, (first, chips) in enumerate(groups):
+        @pl.when(inside[group])
+        def _():
+            waited = chips * cols_n - 1
+            if group < 2:
+                waited += groups[group + 1][1] * cols_n
+            pl.semaphore_wait(barrier, waited)
+
+    def token_copy(group, target, n):
+        part, p = n // lines, (n + line) % lines
+        q = c * local_chunks + part
+        chip, core = chip_of(target, q, p), p % cols_n
+        src = tok_ref.at[pl.ds(part * chunk_rows + p * rows, rows)]
+        dst = tins[target].at[slot(target, q), r]
+        if target == group:
+            dst = tins[target].at[slot(target, q), early[group] + r - groups[group][0]]
+        send = own_send_sem if target == group else next_send_sem
+        recv = own_sem if target == group else early_sem
+        remote = pltpu.make_async_remote_copy(
+            src_ref=src, dst_ref=dst, send_sem=send.at[n], recv_sem=recv.at[q],
+            device_id={"rows": chip, "cols": core}, device_id_type=MESH,
+        )
+        away = (chip != r) | (core != c)
+        return away, remote, lambda: pltpu.make_async_copy(src, dst, recv.at[q])
+
+    def send_own(group, n):
+        away, remote, local = token_copy(group, group, n)
+
+        @pl.when(away)
+        def _():
+            remote.start()
+
+        @pl.when(jnp.logical_not(away))
+        def _():
+            local().start()
+
+    def send_next(group, part):
+        def one(p, _):
+            token_copy(group, group + 1, part * lines + p)[1].start()
+            return 0
+
+        lax.fori_loop(0, lines, one, 0)
+
+    ahead = 2
+    for group in range(3):
+        @pl.when(inside[group])
+        def _():
+            def one_part(part, _):
+                def one(p, _):
+                    send_own(group, part * lines + p)
+                    return 0
+
+                lax.fori_loop(0, lines, one, 0)
+                if group == 0:
+                    send_next(group, part)
+                if group == 1:
+                    @pl.when(c * local_chunks + part < ahead)
+                    def _():
+                        send_next(group, part)
+                return 0
+
+            lax.fori_loop(0, local_chunks, one_part, 0)
+
+    def column_copy(step):
+        other = (c + step) % cols_n
+        return pltpu.make_async_remote_copy(
+            src_ref=tok_ref, dst_ref=tcol.at[c],
+            send_sem=csend_sem.at[step], recv_sem=crecv_sem.at[step],
+            device_id={"cols": other}, device_id_type=MESH,
+        )
+
+    for step in range(1, cols_n):
+        column_copy(step).start()
+
+    def in_order(base, first, count):
+        return jnp.concatenate([
+            order_ref[t, pl.ds(base + first, count, stride=columns), :] for t in range(width // LANES)
+        ], axis=1)
+
+    def keep_order(base, tokens):
+        flat = tokens.astype(jnp.float32).reshape(-1, width)
+        for t in range(width // LANES):
+            order_ref[t, base : base + flat.shape[0]] = flat[:, t * LANES : (t + 1) * LANES]
+
+    def gate_part(core):
+        keep_order(0, tcol[core])
+        for w in range(per_core):
+            normed = normalise(in_order(0, c * per_core + w, height), gain_ref[...])
+            base = pl.multiple_of(w * total + core * height, height)
+            inject = transposed_dot(normed, wbc_ref[2 * states : 3 * states])
+            inject = inject.astype(jnp.bfloat16).astype(jnp.float32)
+            for n in range(states):
+                inject_ref[pl.ds(base * states + n, height, stride=states), :] = jnp.broadcast_to(
+                    inject[:, n : n + 1], (height, LANES)
+                )
+            read = transposed_dot(normed, spread_ref[...])
+            owner = lax.broadcasted_iota(jnp.int32, read.shape, 1) // states
+            here = lax.broadcasted_iota(jnp.int32, read.shape, 0) % run
+            read_ref[pl.ds(base, height), :] = jnp.where(owner == here, read, 0.0).astype(jnp.bfloat16)
+            for k in range(0, inner, LANE_PAIR):
+                z_ref[pl.ds(base, height), k : k + LANE_PAIR] = jnp.dot(
+                    normed, win_ref[:, inner + k : inner + k + LANE_PAIR],
+                    preferred_element_type=jnp.float32,
+                ).astype(jnp.bfloat16)
+
+    for fetch in fetches:
+        fetch.wait()
+
+    for group, (first, chips) in enumerate(groups):
+        @pl.when(inside[group])
+        def _():
+            def fill(d, _):
+                for k in range(pairs):
+                    rate = rrate_ref[:, k * LANE_PAIR : (k + 1) * LANE_PAIR]
+                    table[k, d] = jnp.exp(-rate * d.astype(jnp.float32)).astype(jnp.bfloat16)
+                return 0
+
+            lax.fori_loop(0, (early[group] + chips) * columns, fill, 0)
+
+    for i in range(run):
+        spread_ref[i * states : (i + 1) * states] = wbc_ref[3 * states : 4 * states]
+    crate_ref[...] = jnp.exp(-crate_ref[...])
+    state_ref[...] = jnp.zeros(state_ref.shape, jnp.float32)
+    gate_part(c)
+    for step in range(1, cols_n):
+        column_copy(step).wait_recv()
+        gate_part((c + cols_n - step) % cols_n)
+
+    def relay_copy(q):
+        return pltpu.make_async_remote_copy(
+            src_ref=tin_b.at[q, pl.ds(0, quarter)], dst_ref=tin_c.at[q // 2, pl.ds(0, quarter)],
+            send_sem=relay_sem.at[q], recv_sem=early_sem.at[q],
+            device_id={"rows": r + quarter + q % 2 * quarter}, device_id_type=MESH,
+        )
+
+    def result_copy(group, q, k):
+        first, chips = groups[group]
+        g = ((r - first) * cols_n + c + k) % (chips * cols_n)
+        src, dst = rsend.at[slot(group, q), g], rrecv.at[q, line]
+        remote = pltpu.make_async_remote_copy(
+            src_ref=src, dst_ref=dst, send_sem=rsend_sem.at[slot(group, q), k], recv_sem=rrecv_sem.at[q],
+            device_id={"rows": first + g // cols_n, "cols": g % cols_n}, device_id_type=MESH,
+        )
+        return remote, lambda: pltpu.make_async_copy(src, dst, rrecv_sem.at[q])
+
+    def row_chunk(group, q):
+        chips = groups[group][1]
+        before = early[group]
+        at = slot(group, q)
+        tin = tins[group]
+        if before:
+            part = tin.at[at, pl.ds(0, before)]
+            pltpu.make_async_copy(part, part, early_sem.at[q]).wait()
+        if group == 1:
+            relay_copy(q).start()
+            later = q + ahead
+
+            @pl.when((later < chunks) & (later // local_chunks == c))
+            def _():
+                send_next(group, later % local_chunks)
+        part = tin.at[at, pl.ds(before, chips)]
+        pltpu.make_async_copy(part, part, own_sem.at[q]).wait()
+        out_cols, pre_cols = chips * columns, before * columns
+        all_cols = out_cols + pre_cols
+        block = columns * rows
+        for s in range(before + chips):
+            keep_order(s * block, tin[at, s])
+        for s in range(before + chips):
+            ordered = jnp.concatenate([in_order(s * block, w, rows) for w in range(columns)], axis=0)
+            normed_ref[s * block : (s + 1) * block] = normalise(ordered, gain_ref[...])
+        normed = normed_ref[: all_cols * rows]
+        b_ref[: all_cols * rows] = transposed_dot(normed, wbc_ref[:states]).astype(jnp.bfloat16).astype(jnp.float32)
+        c_ref[: out_cols * rows] = transposed_dot(
+            normed_ref[pre_cols * rows : all_cols * rows], wbc_ref[states : 2 * states]
+        ).astype(jnp.bfloat16).astype(jnp.float32)
+        for k in range(pairs):
+            u_ref[k, : all_cols * rows] = jnp.dot(
+                normed, win_ref[:, k * LANE_PAIR : (k + 1) * LANE_PAIR], preferred_element_type=jnp.float32
+            ).astype(jnp.bfloat16).astype(jnp.float32)
+
+        def span(d):
+            low = max(0, d - pre_cols)
+            return low, out_cols - low, pre_cols + low - d
+
+        for d in range(all_cols):
+            low, count, source = span(d)
+            lag_ref[d, : count * rows] = (
+                c_ref[low * rows : out_cols * rows] * b_ref[source * rows : (source + count) * rows]
+            ).astype(jnp.bfloat16)
+
+        def one_pair(k, _):
+            skip = skip_ref[k]
+            sums = [
+                skip * u_ref[k, (pre_cols + o) * rows : (pre_cols + o + 1) * rows] for o in range(out_cols)
+            ]
+            for d in range(all_cols):
+                low, count, source = span(d)
+                weight = jnp.dot(lag_ref[d, : count * rows], table[k, d], preferred_element_type=jnp.float32)
+                for i in range(count):
+                    sums[low + i] += weight[i * rows : (i + 1) * rows] * u_ref[
+                        k, (source + i) * rows : (source + i + 1) * rows
+                    ]
+            for o in range(out_cols):
+                rsend[at, o // per_core, o % per_core, :, pl.ds(pl.multiple_of(k * LANE_PAIR, LANE_PAIR), LANE_PAIR)] = (
+                    sums[o].astype(jnp.bfloat16)
+                )
+            return 0
+
+        lax.fori_loop(0, pairs, one_pair, 0)
+        result_copy(group, q, 0)[1]().start()
+
+        def send_result(k, _):
+            result_copy(group, q, k)[0].start()
+            return 0
+
+        lax.fori_loop(1, chips * cols_n, send_result, 0)
+
+    def out_copy(q):
+        return pltpu.make_async_remote_copy(
+            src_ref=stage.at[q], dst_ref=land.at[c, q % local_chunks],
+            send_sem=osend_sem.at[q], recv_sem=orecv_sem.at[c, q % local_chunks],
+            device_id={"cols": q // local_chunks}, device_id_type=MESH,
+        )
+
+    def col_chunk(q):
+        pltpu.make_async_copy(rrecv.at[q], rrecv.at[q], rrecv_sem.at[q]).wait()
+        for p in range(lines):
+            for w in range(per_core):
+                value = rrecv[q, p, w].astype(jnp.float32)
+                for t in range(tiles):
+                    vcol[t, w * chunk_rows + p * rows : w * chunk_rows + (p + 1) * rows] = (
+                        value[:, t * LANES : (t + 1) * LANES]
+                    )
+        halves = range(0, states, SUBLANES)
+
+        def one_run(i, _):
+            for w in range(per_core):
+                here = pl.multiple_of(w * chunk_rows + i * run, run)
+                patch = pl.multiple_of(w * total + q * chunk_rows + i * run, run)
+                decay = [[crate_ref[h : h + SUBLANES, t * LANES : (t + 1) * LANES] for t in range(tiles)] for h in halves]
+                state = [[state_ref[w, h : h + SUBLANES, t * LANES : (t + 1) * LANES] for t in range(tiles)] for h in halves]
+                for s in range(run):
+                    inject = [
+                        inject_ref[pl.ds(pl.multiple_of((patch + s) * states + h, SUBLANES), SUBLANES), :] for h in halves
+                    ]
+                    for t in range(tiles):
+                        value = vcol[t, pl.ds(here + s, SUBLANES, stride=0), :]
+                        for j in range(len(inject)):
+                            state[j][t] = decay[j][t] * state[j][t] + inject[j] * value
+                        hist[w, s * states : (s + 1) * states, t * LANES : (t + 1) * LANES] = jnp.concatenate(
+                            [state[j][t] for j in range(len(inject))], axis=0
+                        ).astype(jnp.bfloat16)
+                for j, h in enumerate(halves):
+                    for t in range(tiles):
+                        state_ref[w, h : h + SUBLANES, t * LANES : (t + 1) * LANES] = state[j][t]
+                mixed = jnp.dot(read_ref[pl.ds(patch, run), :], hist[w], preferred_element_type=jnp.float32)
+                for t in range(tiles):
+                    gate = z_ref[pl.ds(patch, run), t * LANES : (t + 1) * LANES].astype(jnp.float32)
+                    both = mixed[:, t * LANES : (t + 1) * LANES] + vcol[t, pl.ds(here, run), :]
+                    gated_ref[pl.ds(here, run), t * LANES : (t + 1) * LANES] = (
+                        both * (gate / (1.0 + jnp.exp(-gate)))
+                    ).astype(jnp.bfloat16)
+            return 0
+
+        lax.fori_loop(0, chunk_rows // run, one_run, 0)
+        result = jnp.dot(gated_ref[...], wout_ref[...], preferred_element_type=jnp.float32).astype(jnp.bfloat16)
+        home = q // local_chunks
+
+        @pl.when(home == c)
+        def _():
+            land[c, q % local_chunks] = result
+
+        @pl.when(home != c)
+        def _():
+            stage[q] = result
+            out_copy(q).start()
+
+    def one_chunk(q, _):
+        for group in range(3):
+            mine = inside[group] & (q < chunks)
+            if group == 2:
+                mine = mine & (q % 2 == (r - 2 * quarter) // quarter)
+
+            @pl.when(mine)
+            def _():
+                row_chunk(group, q)
+
+        @pl.when(q > 0)
+        def _():
+            col_chunk(q - 1)
+        return 0
+
+    lax.fori_loop(0, chunks + 1, one_chunk, 0)
+
+    for group, (first, chips) in enumerate(groups):
+        @pl.when(inside[group])
+        def _():
+            def drain_tokens(n, _):
+                away, remote, _ = token_copy(group, group, n)
+
+                @pl.when(away)
+                def _():
+                    remote.wait_send()
+                if group < 2:
+                    token_copy(group, group + 1, n)[1].wait_send()
+                return 0
+
+            lax.fori_loop(0, local_chunks * lines, drain_tokens, 0)
+
+            def drain_chunk(q, _):
+                if group == 1:
+                    relay_copy(q).wait_send()
+
+                def one(k, _):
+                    result_copy(group, q, k)[0].wait_send()
+                    return 0
+
+                if group == 2:
+                    @pl.when(q % 2 == (r - 2 * quarter) // quarter)
+                    def _():
+                        lax.fori_loop(1, chips * cols_n, one, 0)
+                else:
+                    lax.fori_loop(1, chips * cols_n, one, 0)
+                return 0
+
+            lax.fori_loop(0, chunks, drain_chunk, 0)
+
+    for step in range(1, cols_n):
+        column_copy(step).wait_send()
+
+    def drain_out(q, _):
+        @pl.when(q // local_chunks != c)
+        def _():
+            out_copy(q).wait_send()
+        return 0
+
+    lax.fori_loop(0, chunks, drain_out, 0)
+    for source in range(cols_n):
+        @pl.when(source != c)
+        def _():
+            for i in range(local_chunks):
+                pltpu.make_async_copy(
+                    land.at[source, i], land.at[source, i], orecv_sem.at[source, i]
+                ).wait()
+    for source in range(cols_n):
+        for i in range(local_chunks):
+            for w in range(per_core):
+                out_ref[source * per_core + w, i * chunk_rows : (i + 1) * chunk_rows] = (
+                    land[source, i, w * chunk_rows : (w + 1) * chunk_rows]
+                )
+
+
+def per_device_grouped(chunks, tokens, norm_gain, w_in, w_bc, rate_row, rate_col, skip_gain, w_out):
+    inner, width_out = w_out.shape
+    states = rate_row.shape[0]
+    height, columns, width = tokens.shape
+    rows_n, cols_n = lax.axis_size("rows"), lax.axis_size("cols")
+    quarter = rows_n // 4
+    per_core = columns // cols_n
+    total = height * cols_n
+    chunk_rows = total // chunks
+    lines = quarter * cols_n
+    rows = chunk_rows // lines
+    tiles = inner // LANES
+    pairs = inner // LANE_PAIR
+    patches = total * per_core
+    local_chunks = chunks // cols_n
+    lags = rows_n * columns
+    held = lags * rows
+    outs = 2 * quarter * columns * rows
+    f32, bf16 = jnp.float32, jnp.bfloat16
+    dma = pltpu.SemaphoreType.DMA
+    out = pl.pallas_call(
+        functools.partial(grouped_kernel, states, rows_n, cols_n, chunks, per_core),
+        in_specs=[pl.BlockSpec(memory_space=pl.ANY)] * 8,
+        out_specs=pl.BlockSpec(memory_space=pltpu.VMEM),
+        out_shape=jax.ShapeDtypeStruct((columns, height, width_out), bf16),
+        scratch_shapes=[
+            pltpu.VMEM((1, width), f32),
+            pltpu.VMEM(w_in.shape, bf16),
+            pltpu.VMEM(w_bc.shape[::-1], bf16),
+            pltpu.VMEM(rate_row.shape, f32),
+            pltpu.VMEM(rate_col.shape, f32),
+            pltpu.VMEM((pairs, 1, LANE_PAIR), f32),
+            pltpu.VMEM(w_out.shape, bf16),
+            pltpu.VMEM((cols_n, height, columns, width), bf16),
+            pltpu.VMEM((chunks, quarter, rows, columns, width), bf16),
+            pltpu.VMEM((chunks, 2 * quarter, rows, columns, width), bf16),
+            pltpu.VMEM((chunks // 2, 4 * quarter, rows, columns, width), bf16),
+            pltpu.VMEM((pairs, lags, states, LANE_PAIR), bf16),
+            pltpu.VMEM((width // LANES, max(held, height * columns), LANES), f32),
+            pltpu.VMEM((held, width), bf16),
+            pltpu.VMEM((pairs, held, LANE_PAIR), f32),
+            pltpu.VMEM((held, states), f32),
+            pltpu.VMEM((outs, states), f32),
+            pltpu.VMEM((lags, outs, states), bf16),
+            pltpu.VMEM((chunks, 2 * lines, per_core, rows, inner), bf16),
+            pltpu.VMEM((chunks, lines, per_core, rows, inner), bf16),
+            pltpu.VMEM((tiles, per_core * chunk_rows + SUBLANES, LANES), f32),
+            pltpu.VMEM((patches * states, LANES), f32),
+            pltpu.VMEM((LANE_PAIR, width), bf16),
+            pltpu.VMEM((patches, LANE_PAIR), bf16),
+            pltpu.VMEM((per_core, LANE_PAIR, inner), bf16),
+            pltpu.VMEM((patches, inner), bf16),
+            pltpu.VMEM((per_core * chunk_rows, inner), bf16),
+            pltpu.VMEM((chunks, per_core * chunk_rows, width_out), bf16),
+            pltpu.VMEM((cols_n, local_chunks, per_core * chunk_rows, width_out), bf16),
+            pltpu.VMEM((per_core, states, inner), f32),
+            dma((local_chunks * lines,)), dma((local_chunks * lines,)), dma((chunks,)), dma((chunks,)), dma((chunks,)),
+            dma((cols_n,)), dma((cols_n,)),
+            dma((chunks, 2 * lines)), dma((chunks,)), dma((chunks,)),
+            dma((cols_n, local_chunks)), dma((8,)),
+        ],
+        compiler_params=pltpu.CompilerParams(
+            vmem_limit_bytes=VMEM_LIMIT, collective_id=0, has_side_effects=True
+        ),
+        name="layer",
+    )(
+        tokens, norm_gain[None], w_in, w_bc.T, rate_row, rate_col,
+        skip_gain.reshape(pairs, 1, LANE_PAIR), w_out,
+    )
+    return out.transpose(1, 0, 2)
+
+
+def chunk_count(tokens, rate_row, inner):
+    height, columns, _ = tokens.shape
+    states = rate_row.shape[0]
+    rows_n, cols_n = lax.axis_size("rows"), lax.axis_size("cols")
+    total = height * cols_n
+    if rows_n % 4 or columns % cols_n or inner % LANE_PAIR or states % SUBLANES or LANE_PAIR % states:
+        return 0
+    step = rows_n // 4 * cols_n * SUBLANES
+    run = LANE_PAIR // states
+    if total % step or step % run or total // step % (2 * cols_n):
+        return 0
+    return total // step
+
+
+def per_device(tokens, norm_gain, w_in, w_bc, rate_row, rate_col, skip_gain, w_out):
+    args = (tokens, norm_gain, w_in, w_bc, rate_row, rate_col, skip_gain, w_out)
+    chunks = chunk_count(tokens, rate_row, w_out.shape[0])
+    if chunks:
+        return per_device_grouped(chunks, *args)
+    return per_device_uniform(*args)
+
+
 def solution(mesh):
     placed = (P(("slides", "cols"), "rows", None), P(), P(), P(), P(), P(), P(), P())
     return jax.shard_map(

time: 47.7 us -> 57.7 us (1.21)
  the two profiles are of different devices: /device:TPU:0 before, /device:TPU:17 now
where the time goes in v2:
time: 57.7 us; the launch traced here: 57.3 us
  Pallas kernels  55.1 us (95%)
  local copies, waits for them, and re-layouts  2.24 us (4%)
    pallas_call x1, Pallas kernels, per_device_grouped(): pl.pallas_call(functools.partial(grouped_kernel, states, rows_n, cols_n,...  55.1 us
    transpose x1, local copies, waits for them, and re-layouts, per_device_grouped(): return out.transpose(1, 0, 2)  2.24 us

profile of v2, /device:TPU:17, one launch (start us, length us, event | category | flops | bytes accessed | tf_op | source)
XLA Modules:
  0.0 57.3 jit_solution(2117515877407792404)
XLA Ops:
  0.0 55.1 %layer.1 = bf16[4,128,512]{2,1,0:T(8,128)(2,1)} custom-call(bf16[128,4,512]{2,1,0:T(4,128)(2,1)} %tok_ref.1, f32[1,512]{1,0:T(1,128)} %bitcast.7, bf16[512,2048]{1,0:T(8,128)(2,1)} %win_in.1, bf16[64,512]{1,0:T(8,128)(2,1)} %bitcast.5, f32[16,1024]{1,0:T(8,128)} %rrate_in.1, f32[16,1024]{1,0:T(8,128)} %crate_in.1, f32[4,1,256]{2,1,0:T(1,128)} %bitcast.6, ...), custom_call_target="tpu_custom_call" | custom-call | tf_op jit(solution)/shard_map/layer/pallas_call | solution.py:836
  55.1 2.2 %copy.9 = bf16[128,4,512]{2,1,0:T(4,128)(2,1)} copy(bf16[128,4,512]{2,0,1:T(8,128)(2,1)} %bitcast.4) | data formatting | bytes 1048576 | tf_op jit(solution)/shard_map/transpose | solution.py:885

commit v3 on v2

--- a/solution.py
+++ b/solution.py
@@ -396,9 +396,9 @@
     tok_ref, gain_in, win_in, wbc_in, rrate_in, crate_in, skip_in, wout_in,
     out_ref,
     gain_ref, win_ref, wbc_ref, rrate_ref, crate_ref, skip_ref, wout_ref,
-    tcol, tin_a, tin_b, tin_c, table, order_ref, normed_ref, u_ref, b_ref, c_ref, lag_ref,
+    tokv, nown, ncol, tin_a, tin_b, tin_c, table, order_ref, u_ref, b_ref, c_ref, lag_ref,
     rsend, rrecv, vcol, inject_ref, spread_ref, read_ref, hist, z_ref, gated_ref, stage, land, state_ref,
-    own_send_sem, next_send_sem, own_sem, early_sem, relay_sem, csend_sem, crecv_sem, rsend_sem, rrecv_sem,
+    own_send_sem, own_sem, early_sem, relay_sem, csend_sem, crecv_sem, rsend_sem, rrecv_sem,
     osend_sem, orecv_sem, fetch_sem,
 ):
     height, columns, width = tok_ref.shape
@@ -412,6 +412,8 @@
     lines = quarter * cols_n
     rows = chunk_rows // lines
     run = LANE_PAIR // states
+    parts = rsend_sem.shape[1]
+    share = inner // parts
     r, c = lax.axis_index("rows"), lax.axis_index("cols")
 
     groups = ((0, quarter), (quarter, quarter), (2 * quarter, 2 * quarter))
@@ -445,89 +447,73 @@
 
             lax.fori_loop(0, chips * cols_n, one, 0)
             if group:
-                def back(k, _):
-                    greet(first - quarter + k // cols_n, k % cols_n)
-                    return 0
-
-                lax.fori_loop(0, lines, back, 0)
+                greet(first - quarter + (r - first) % quarter, c)
 
     fetches = [
         pltpu.make_async_copy(src, dst, fetch_sem.at[k])
         for k, (src, dst) in enumerate((
-            (rrate_in, rrate_ref), (crate_in, crate_ref), (skip_in, skip_ref), (gain_in, gain_ref),
-            (wbc_in, wbc_ref), (tok_ref, tcol.at[c]), (win_in, win_ref), (wout_in, wout_ref),
+            (tok_ref, tokv), (gain_in, gain_ref), (rrate_in, rrate_ref), (crate_in, crate_ref),
+            (skip_in, skip_ref), (wbc_in, wbc_ref), (win_in, win_ref), (wout_in, wout_ref),
         ))
     ]
     for fetch in fetches:
         fetch.start()
+    for fetch in fetches[:2]:
+        fetch.wait()
+    for first in range(0, height, chunk_rows):
+        flat = normalise(tokv[first : first + chunk_rows].astype(jnp.float32).reshape(-1, width), gain_ref[...])
+        flat = flat.astype(jnp.float32)
+        for t in range(width // LANES):
+            order_ref[t, first * columns : (first + chunk_rows) * columns] = flat[:, t * LANES : (t + 1) * LANES]
+        for w in range(columns):
+            nown[w, first : first + chunk_rows] = jnp.concatenate([
+                order_ref[t, pl.ds(first * columns + w, chunk_rows, stride=columns), :] for t in range(width // LANES)
+            ], axis=1).astype(jnp.bfloat16)
 
     for group, (first, chips) in enumerate(groups):
         @pl.when(inside[group])
         def _():
-            waited = chips * cols_n - 1
-            if group < 2:
-                waited += groups[group + 1][1] * cols_n
-            pl.semaphore_wait(barrier, waited)
-
-    def token_copy(group, target, n):
+            pl.semaphore_wait(barrier, chips * cols_n - 1 + (1, 2, 0)[group])
+
+    def token_copy(group, n):
         part, p = n // lines, (n + line) % lines
         q = c * local_chunks + part
-        chip, core = chip_of(target, q, p), p % cols_n
-        src = tok_ref.at[pl.ds(part * chunk_rows + p * rows, rows)]
-        dst = tins[target].at[slot(target, q), r]
-        if target == group:
-            dst = tins[target].at[slot(target, q), early[group] + r - groups[group][0]]
-        send = own_send_sem if target == group else next_send_sem
-        recv = own_sem if target == group else early_sem
+        chip, core = chip_of(group, q, p), p % cols_n
+        src = nown.at[:, pl.ds(pl.multiple_of(part * chunk_rows + p * rows, rows), rows)]
+        dst = tins[group].at[slot(group, q), early[group] + r - groups[group][0]]
         remote = pltpu.make_async_remote_copy(
-            src_ref=src, dst_ref=dst, send_sem=send.at[n], recv_sem=recv.at[q],
+            src_ref=src, dst_ref=dst, send_sem=own_send_sem.at[n], recv_sem=own_sem.at[q],
             device_id={"rows": chip, "cols": core}, device_id_type=MESH,
         )
         away = (chip != r) | (core != c)
-        return away, remote, lambda: pltpu.make_async_copy(src, dst, recv.at[q])
-
-    def send_own(group, n):
-        away, remote, local = token_copy(group, group, n)
-
-        @pl.when(away)
-        def _():
-            remote.start()
-
-        @pl.when(jnp.logical_not(away))
-        def _():
-            local().start()
-
-    def send_next(group, part):
-        def one(p, _):
-            token_copy(group, group + 1, part * lines + p)[1].start()
-            return 0
-
-        lax.fori_loop(0, lines, one, 0)
-
-    ahead = 2
-    for group in range(3):
-        @pl.when(inside[group])
-        def _():
-            def one_part(part, _):
-                def one(p, _):
-                    send_own(group, part * lines + p)
+        return away, remote, lambda: pltpu.make_async_copy(src, dst, own_sem.at[q])
+
+    def send_own(low, high):
+        for group in range(3):
+            @pl.when(inside[group])
+            def _():
+                def one(n, _):
+                    away, remote, local = token_copy(group, n)
+
+                    @pl.when(away)
+                    def _():
+                        remote.start()
+
+                    @pl.when(jnp.logical_not(away))
+                    def _():
+                        local().start()
                     return 0
 
-                lax.fori_loop(0, lines, one, 0)
-                if group == 0:
-                    send_next(group, part)
-                if group == 1:
-                    @pl.when(c * local_chunks + part < ahead)
-                    def _():
-                        send_next(group, part)
-                return 0
-
-            lax.fori_loop(0, local_chunks, one_part, 0)
+                lax.fori_loop(low * lines, high * lines, one, 0)
+
+    @pl.when(c == 0)
+    def _():
+        send_own(0, 1)
 
     def column_copy(step):
         other = (c + step) % cols_n
         return pltpu.make_async_remote_copy(
-            src_ref=tok_ref, dst_ref=tcol.at[c],
+            src_ref=nown.at[pl.ds(other * per_core, per_core)], dst_ref=ncol.at[c],
             send_sem=csend_sem.at[step], recv_sem=crecv_sem.at[step],
             device_id={"cols": other}, device_id_type=MESH,
         )
@@ -535,20 +521,37 @@
     for step in range(1, cols_n):
         column_copy(step).start()
 
-    def in_order(base, first, count):
-        return jnp.concatenate([
-            order_ref[t, pl.ds(base + first, count, stride=columns), :] for t in range(width // LANES)
-        ], axis=1)
-
-    def keep_order(base, tokens):
-        flat = tokens.astype(jnp.float32).reshape(-1, width)
-        for t in range(width // LANES):
-            order_ref[t, base : base + flat.shape[0]] = flat[:, t * LANES : (t + 1) * LANES]
-
-    def gate_part(core):
-        keep_order(0, tcol[core])
+    def own_wait(group, q):
+        part = tins[group].at[slot(group, q), pl.ds(early[group], groups[group][1])]
+        pltpu.make_async_copy(part, part, own_sem.at[q]).wait()
+
+    def early_wait(group, q):
+        part = tins[group].at[slot(group, q), pl.ds(0, early[group])]
+        pltpu.make_async_copy(part, part, early_sem.at[q]).wait()
+
+    def relay_copy(group, q, which):
+        if group == 0:
+            src, dst, chip = tin_a.at[q], tin_b.at[q, pl.ds(0, quarter)], r + quarter
+        else:
+            src = tin_b.at[q, pl.ds(which * quarter, quarter)]
+            dst = tin_c.at[q // 2, pl.ds(which * quarter, quarter)]
+            chip = r + quarter + q % 2 * quarter
+        return pltpu.make_async_remote_copy(
+            src_ref=src, dst_ref=dst, send_sem=relay_sem.at[q, which], recv_sem=early_sem.at[q],
+            device_id={"rows": chip}, device_id_type=MESH,
+        )
+
+    def relay_own(group, q):
+        own_wait(group, q)
+        relay_copy(group, q, 1).start()
+
+    def relay_early(group, q):
+        early_wait(group, q)
+        relay_copy(group, q, 0).start()
+
+    def gate_part(core, normed_of):
         for w in range(per_core):
-            normed = normalise(in_order(0, c * per_core + w, height), gain_ref[...])
+            normed = normed_of(w)
             base = pl.multiple_of(w * total + core * height, height)
             inject = transposed_dot(normed, wbc_ref[2 * states : 3 * states])
             inject = inject.astype(jnp.bfloat16).astype(jnp.float32)
@@ -566,7 +569,7 @@
                     preferred_element_type=jnp.float32,
                 ).astype(jnp.bfloat16)
 
-    for fetch in fetches:
+    for fetch in fetches[2:]:
         fetch.wait()
 
     for group, (first, chips) in enumerate(groups):
@@ -584,24 +587,57 @@
         spread_ref[i * states : (i + 1) * states] = wbc_ref[3 * states : 4 * states]
     crate_ref[...] = jnp.exp(-crate_ref[...])
     state_ref[...] = jnp.zeros(state_ref.shape, jnp.float32)
-    gate_part(c)
+    @pl.when(c == 0)
+    def _():
+        send_own(1, 2)
+
+    @pl.when(inside[0])
+    def _():
+        relay_own(0, 0)
+
+    gate_part(c, lambda w: nown[c * per_core + w])
+
+    @pl.when(c == 0)
+    def _():
+        send_own(2, local_chunks)
+
+    @pl.when(inside[0])
+    def _():
+        relay_own(0, 1)
+
+    @pl.when(inside[1])
+    def _():
+        relay_own(1, 0)
+
     for step in range(1, cols_n):
         column_copy(step).wait_recv()
-        gate_part((c + cols_n - step) % cols_n)
-
-    def relay_copy(q):
-        return pltpu.make_async_remote_copy(
-            src_ref=tin_b.at[q, pl.ds(0, quarter)], dst_ref=tin_c.at[q // 2, pl.ds(0, quarter)],
-            send_sem=relay_sem.at[q], recv_sem=early_sem.at[q],
-            device_id={"rows": r + quarter + q % 2 * quarter}, device_id_type=MESH,
-        )
-
-    def result_copy(group, q, k):
+        source = (c + cols_n - step) % cols_n
+        gate_part(source, lambda w: ncol[source, w])
+
+    @pl.when(c > 0)
+    def _():
+        send_own(0, local_chunks)
+
+    @pl.when(inside[0])
+    def _():
+        def one(q, _):
+            relay_own(0, q)
+            return 0
+
+        lax.fori_loop(2, local_chunks, one, 0)
+
+    @pl.when(inside[1])
+    def _():
+        relay_early(1, 0)
+        relay_own(1, 1)
+
+    def result_copy(group, q, part, k):
         first, chips = groups[group]
         g = ((r - first) * cols_n + c + k) % (chips * cols_n)
-        src, dst = rsend.at[slot(group, q), g], rrecv.at[q, line]
+        some = pl.ds(pl.multiple_of(part * share, share), share)
+        src, dst = rsend.at[slot(group, q), g, :, :, some], rrecv.at[q, line, :, :, some]
         remote = pltpu.make_async_remote_copy(
-            src_ref=src, dst_ref=dst, send_sem=rsend_sem.at[slot(group, q), k], recv_sem=rrecv_sem.at[q],
+            src_ref=src, dst_ref=dst, send_sem=rsend_sem.at[slot(group, q), part, k], recv_sem=rrecv_sem.at[q],
             device_id={"rows": first + g // cols_n, "cols": g % cols_n}, device_id_type=MESH,
         )
         return remote, lambda: pltpu.make_async_copy(src, dst, rrecv_sem.at[q])
@@ -611,30 +647,15 @@
         before = early[group]
         at = slot(group, q)
         tin = tins[group]
-        if before:
-            part = tin.at[at, pl.ds(0, before)]
-            pltpu.make_async_copy(part, part, early_sem.at[q]).wait()
-        if group == 1:
-            relay_copy(q).start()
-            later = q + ahead
-
-            @pl.when((later < chunks) & (later // local_chunks == c))
-            def _():
-                send_next(group, later % local_chunks)
-        part = tin.at[at, pl.ds(before, chips)]
-        pltpu.make_async_copy(part, part, own_sem.at[q]).wait()
+        if group == 2:
+            early_wait(group, q)
+            own_wait(group, q)
         out_cols, pre_cols = chips * columns, before * columns
         all_cols = out_cols + pre_cols
-        block = columns * rows
-        for s in range(before + chips):
-            keep_order(s * block, tin[at, s])
-        for s in range(before + chips):
-            ordered = jnp.concatenate([in_order(s * block, w, rows) for w in range(columns)], axis=0)
-            normed_ref[s * block : (s + 1) * block] = normalise(ordered, gain_ref[...])
-        normed = normed_ref[: all_cols * rows]
+        normed = tin[at].reshape(all_cols * rows, width)
         b_ref[: all_cols * rows] = transposed_dot(normed, wbc_ref[:states]).astype(jnp.bfloat16).astype(jnp.float32)
         c_ref[: out_cols * rows] = transposed_dot(
-            normed_ref[pre_cols * rows : all_cols * rows], wbc_ref[states : 2 * states]
+            normed[pre_cols * rows :], wbc_ref[states : 2 * states]
         ).astype(jnp.bfloat16).astype(jnp.float32)
         for k in range(pairs):
             u_ref[k, : all_cols * rows] = jnp.dot(
@@ -651,7 +672,7 @@
                 c_ref[low * rows : out_cols * rows] * b_ref[source * rows : (source + count) * rows]
             ).astype(jnp.bfloat16)
 
-        def one_pair(k, _):
+        def one_pair(k):
             skip = skip_ref[k]
             sums = [
                 skip * u_ref[k, (pre_cols + o) * rows : (pre_cols + o + 1) * rows] for o in range(out_cols)
@@ -663,20 +684,23 @@
                     sums[low + i] += weight[i * rows : (i + 1) * rows] * u_ref[
                         k, (source + i) * rows : (source + i + 1) * rows
                     ]
+            some = pl.ds(pl.multiple_of(k * LANE_PAIR, LANE_PAIR), LANE_PAIR)
             for o in range(out_cols):
-                rsend[at, o // per_core, o % per_core, :, pl.ds(pl.multiple_of(k * LANE_PAIR, LANE_PAIR), LANE_PAIR)] = (
-                    sums[o].astype(jnp.bfloat16)
-                )
+                rsend[at, o // per_core, o % per_core, :, some] = sums[o].astype(jnp.bfloat16)
+
+        def one_part(part, _):
+            for k in range(pairs // parts):
+                one_pair(part * (pairs // parts) + k)
+            result_copy(group, q, part, 0)[1]().start()
+
+            def send_result(k, _):
+                result_copy(group, q, part, k)[0].start()
+                return 0
+
+            lax.fori_loop(1, chips * cols_n, send_result, 0)
             return 0
 
-        lax.fori_loop(0, pairs, one_pair, 0)
-        result_copy(group, q, 0)[1]().start()
-
-        def send_result(k, _):
-            result_copy(group, q, k)[0].start()
-            return 0
-
-        lax.fori_loop(1, chips * cols_n, send_result, 0)
+        lax.fori_loop(0, parts, one_part, 0)
 
     def out_copy(q):
         return pltpu.make_async_remote_copy(
@@ -696,9 +720,9 @@
                     )
         halves = range(0, states, SUBLANES)
 
-        def one_run(i, _):
+        def one_run(i):
             for w in range(per_core):
-                here = pl.multiple_of(w * chunk_rows + i * run, run)
+                here = w * chunk_rows + i * run
                 patch = pl.multiple_of(w * total + q * chunk_rows + i * run, run)
                 decay = [[crate_ref[h : h + SUBLANES, t * LANES : (t + 1) * LANES] for t in range(tiles)] for h in halves]
                 state = [[state_ref[w, h : h + SUBLANES, t * LANES : (t + 1) * LANES] for t in range(tiles)] for h in halves]
@@ -710,22 +734,26 @@
                         value = vcol[t, pl.ds(here + s, SUBLANES, stride=0), :]
                         for j in range(len(inject)):
                             state[j][t] = decay[j][t] * state[j][t] + inject[j] * value
-                        hist[w, s * states : (s + 1) * states, t * LANES : (t + 1) * LANES] = jnp.concatenate(
+                        hist[i * per_core + w, t, s * states : (s + 1) * states, :] = jnp.concatenate(
                             [state[j][t] for j in range(len(inject))], axis=0
                         ).astype(jnp.bfloat16)
                 for j, h in enumerate(halves):
                     for t in range(tiles):
                         state_ref[w, h : h + SUBLANES, t * LANES : (t + 1) * LANES] = state[j][t]
-                mixed = jnp.dot(read_ref[pl.ds(patch, run), :], hist[w], preferred_element_type=jnp.float32)
                 for t in range(tiles):
+                    if t % 2 == 0:
+                        both_tiles = jnp.concatenate([hist[i * per_core + w, t], hist[i * per_core + w, t + 1]], axis=1)
+                        mixed = jnp.dot(
+                            read_ref[pl.ds(patch, run), :], both_tiles, preferred_element_type=jnp.float32
+                        )
                     gate = z_ref[pl.ds(patch, run), t * LANES : (t + 1) * LANES].astype(jnp.float32)
-                    both = mixed[:, t * LANES : (t + 1) * LANES] + vcol[t, pl.ds(here, run), :]
+                    both = mixed[:, t % 2 * LANES : (t % 2 + 1) * LANES] + vcol[t, pl.ds(here, run), :]
                     gated_ref[pl.ds(here, run), t * LANES : (t + 1) * LANES] = (
                         both * (gate / (1.0 + jnp.exp(-gate)))
                     ).astype(jnp.bfloat16)
-            return 0
-
-        lax.fori_loop(0, chunk_rows // run, one_run, 0)
+
+        for i in range(chunk_rows // run):
+            one_run(i)
         result = jnp.dot(gated_ref[...], wout_ref[...], preferred_element_type=jnp.float32).astype(jnp.bfloat16)
         home = q // local_chunks
 
@@ -748,34 +776,49 @@
             def _():
                 row_chunk(group, q)
 
-        @pl.when(q > 0)
-        def _():
-            col_chunk(q - 1)
+            if group == 0:
+                @pl.when(inside[group] & (q + local_chunks < chunks))
+                def _():
+                    relay_own(group, q + local_chunks)
+            if group == 1:
+                @pl.when(inside[group] & (q + 1 < chunks))
+                def _():
+                    relay_early(group, q + 1)
+
+                @pl.when(inside[group] & (q + 2 < chunks))
+                def _():
+                    relay_own(group, q + 2)
+
+        @pl.when(q >= lag)
+        def _():
+            col_chunk(q - lag)
         return 0
 
-    lax.fori_loop(0, chunks + 1, one_chunk, 0)
+    lag = 2
+    lax.fori_loop(0, chunks + lag, one_chunk, 0)
 
     for group, (first, chips) in enumerate(groups):
         @pl.when(inside[group])
         def _():
             def drain_tokens(n, _):
-                away, remote, _ = token_copy(group, group, n)
+                away, remote, _ = token_copy(group, n)
 
                 @pl.when(away)
                 def _():
                     remote.wait_send()
+                return 0
+
+            lax.fori_loop(0, local_chunks * lines, drain_tokens, 0)
+
+            def drain_chunk(q, _):
                 if group < 2:
-                    token_copy(group, group + 1, n)[1].wait_send()
-                return 0
-
-            lax.fori_loop(0, local_chunks * lines, drain_tokens, 0)
-
-            def drain_chunk(q, _):
+                    relay_copy(group, q, 1).wait_send()
                 if group == 1:
-                    relay_copy(q).wait_send()
+                    relay_copy(group, q, 0).wait_send()
 
                 def one(k, _):
-                    result_copy(group, q, k)[0].wait_send()
+                    for part in range(parts):
+                        result_copy(group, q, part, k)[0].wait_send()
                     return 0
 
                 if group == 2:
@@ -846,13 +889,14 @@
             pltpu.VMEM(rate_col.shape, f32),
             pltpu.VMEM((pairs, 1, LANE_PAIR), f32),
             pltpu.VMEM(w_out.shape, bf16),
-            pltpu.VMEM((cols_n, height, columns, width), bf16),
-            pltpu.VMEM((chunks, quarter, rows, columns, width), bf16),
-            pltpu.VMEM((chunks, 2 * quarter, rows, columns, width), bf16),
-            pltpu.VMEM((chunks // 2, 4 * quarter, rows, columns, width), bf16),
+            pltpu.VMEM((height, columns, width), bf16),
+            pltpu.VMEM((columns, height, width), bf16),
+            pltpu.VMEM((cols_n, per_core, height, width), bf16),
+            pltpu.VMEM((chunks, quarter, columns, rows, width), bf16),
+            pltpu.VMEM((chunks, 2 * quarter, columns, rows, width), bf16),
+            pltpu.VMEM((chunks // 2, 4 * quarter, columns, rows, width), bf16),
             pltpu.VMEM((pairs, lags, states, LANE_PAIR), bf16),
-            pltpu.VMEM((width // LANES, max(held, height * columns), LANES), f32),
-            pltpu.VMEM((held, width), bf16),
+            pltpu.VMEM((width // LANES, height * columns, LANES), f32),
             pltpu.VMEM((pairs, held, LANE_PAIR), f32),
             pltpu.VMEM((held, states), f32),
             pltpu.VMEM((outs, states), f32),
@@ -863,15 +907,15 @@
             pltpu.VMEM((patches * states, LANES), f32),
             pltpu.VMEM((LANE_PAIR, width), bf16),
             pltpu.VMEM((patches, LANE_PAIR), bf16),
-            pltpu.VMEM((per_core, LANE_PAIR, inner), bf16),
+            pltpu.VMEM((per_core * chunk_rows * states // LANE_PAIR, tiles, LANE_PAIR, LANES), bf16),
             pltpu.VMEM((patches, inner), bf16),
             pltpu.VMEM((per_core * chunk_rows, inner), bf16),
             pltpu.VMEM((chunks, per_core * chunk_rows, width_out), bf16),
             pltpu.VMEM((cols_n, local_chunks, per_core * chunk_rows, width_out), bf16),
             pltpu.VMEM((per_core, states, inner), f32),
-            dma((local_chunks * lines,)), dma((local_chunks * lines,)), dma((chunks,)), dma((chunks,)), dma((chunks,)),
+            dma((local_chunks * lines,)), dma((chunks,)), dma((chunks,)), dma((chunks, 2)),
             dma((cols_n,)), dma((cols_n,)),
-            dma((chunks, 2 * lines)), dma((chunks,)), dma((chunks,)),
+            dma((chunks, 2, 2 * lines)), dma((chunks,)), dma((chunks,)),
             dma((cols_n, local_chunks)), dma((8,)),
         ],
         compiler_params=pltpu.CompilerParams(

time: 57.7 us -> 47 us (0.81)
  Pallas kernels: 55.1 us -> 44.6 us
    pallas_call x1, Pallas kernels: 55.1 us -> 44.6 us  [per_device_grouped(): pl.pallas_call(functools.partial(grouped_kernel, states, rows_n, cols_n,...]
where the time goes in v3:
time: 47 us; the launch traced here: 46.9 us
  Pallas kernels  44.6 us (95%)
  local copies, waits for them, and re-layouts  2.24 us (5%)
    pallas_call x1, Pallas kernels, per_device_grouped(): pl.pallas_call(functools.partial(grouped_kernel, states, rows_n, cols_n,...  44.6 us
    transpose x1, local copies, waits for them, and re-layouts, per_device_grouped(): return out.transpose(1, 0, 2)  2.24 us

profile of v3, /device:TPU:17, one launch (start us, length us, event | category | flops | bytes accessed | tf_op | source)
XLA Modules:
  0.0 46.9 jit_solution(8061600426614974947)
XLA Ops:
  0.0 44.6 %layer.1 = bf16[4,128,512]{2,1,0:T(8,128)(2,1)} custom-call(bf16[128,4,512]{2,1,0:T(4,128)(2,1)} %tok_ref.1, f32[1,512]{1,0:T(1,128)} %bitcast.7, bf16[512,2048]{1,0:T(8,128)(2,1)} %win_in.1, bf16[64,512]{1,0:T(8,128)(2,1)} %bitcast.5, f32[16,1024]{1,0:T(8,128)} %rrate_in.1, f32[16,1024]{1,0:T(8,128)} %crate_in.1, f32[4,1,256]{2,1,0:T(1,128)} %bitcast.6, ...), custom_call_target="tpu_custom_call" | custom-call | tf_op jit(solution)/shard_map/layer/pallas_call | solution.py:879
  44.6 2.2 %copy.9 = bf16[128,4,512]{2,1,0:T(4,128)(2,1)} copy(bf16[128,4,512]{2,0,1:T(8,128)(2,1)} %bitcast.4) | data formatting | bytes 1048576 | tf_op jit(solution)/shard_map/transpose | solution.py:929

commit v4 on v3

--- a/solution.py
+++ b/solution.py
@@ -399,7 +399,7 @@
     tokv, nown, ncol, tin_a, tin_b, tin_c, table, order_ref, u_ref, b_ref, c_ref, lag_ref,
     rsend, rrecv, vcol, inject_ref, spread_ref, read_ref, hist, z_ref, gated_ref, stage, land, state_ref,
     own_send_sem, own_sem, early_sem, relay_sem, csend_sem, crecv_sem, rsend_sem, rrecv_sem,
-    osend_sem, orecv_sem, fetch_sem,
+    osend_sem, orecv_sem, fetch_sem, ready_sem,
 ):
     height, columns, width = tok_ref.shape
     inner = wout_ref.shape[0]
@@ -446,21 +446,24 @@
                 return 0
 
             lax.fori_loop(0, chips * cols_n, one, 0)
-            if group:
-                greet(first - quarter + (r - first) % quarter, c)
-
+            if group < 2:
+                for k in range(group + 1):
+                    greet(r + (k + 1) * quarter, c)
+
+    head, rest = pl.ds(0, chunk_rows), pl.ds(chunk_rows, height - chunk_rows)
     fetches = [
         pltpu.make_async_copy(src, dst, fetch_sem.at[k])
         for k, (src, dst) in enumerate((
-            (tok_ref, tokv), (gain_in, gain_ref), (rrate_in, rrate_ref), (crate_in, crate_ref),
-            (skip_in, skip_ref), (wbc_in, wbc_ref), (win_in, win_ref), (wout_in, wout_ref),
+            (tok_ref.at[head], tokv.at[head]), (gain_in, gain_ref), (tok_ref.at[rest], tokv.at[rest]),
+            (rrate_in, rrate_ref), (wbc_in, wbc_ref), (win_in, win_ref),
+            (crate_in, crate_ref), (skip_in, skip_ref), (wout_in, wout_ref),
         ))
     ]
     for fetch in fetches:
         fetch.start()
-    for fetch in fetches[:2]:
-        fetch.wait()
-    for first in range(0, height, chunk_rows):
+
+    def normalise_part(part):
+        first = part * chunk_rows
         flat = normalise(tokv[first : first + chunk_rows].astype(jnp.float32).reshape(-1, width), gain_ref[...])
         flat = flat.astype(jnp.float32)
         for t in range(width // LANES):
@@ -470,10 +473,18 @@
                 order_ref[t, pl.ds(first * columns + w, chunk_rows, stride=columns), :] for t in range(width // LANES)
             ], axis=1).astype(jnp.bfloat16)
 
+    for fetch in fetches[:2]:
+        fetch.wait()
+    normalise_part(0)
+
     for group, (first, chips) in enumerate(groups):
         @pl.when(inside[group])
         def _():
-            pl.semaphore_wait(barrier, chips * cols_n - 1 + (1, 2, 0)[group])
+            pl.semaphore_wait(barrier, chips * cols_n - 1 + (group > 0))
+            if group:
+                pl.semaphore_signal(
+                    ready_sem, inc=1, device_id={"rows": first - quarter + (r - first) % quarter}, device_id_type=MESH
+                )
 
     def token_copy(group, n):
         part, p = n // lines, (n + line) % lines
@@ -509,6 +520,10 @@
     @pl.when(c == 0)
     def _():
         send_own(0, 1)
+
+    fetches[2].wait()
+    for part in range(1, local_chunks):
+        normalise_part(part)
 
     def column_copy(step):
         other = (c + step) % cols_n
@@ -569,7 +584,7 @@
                     preferred_element_type=jnp.float32,
                 ).astype(jnp.bfloat16)
 
-    for fetch in fetches[2:]:
+    for fetch in fetches[3:]:
         fetch.wait()
 
     for group, (first, chips) in enumerate(groups):
@@ -593,6 +608,7 @@
 
     @pl.when(inside[0])
     def _():
+        pl.semaphore_wait(ready_sem, 1)
         relay_own(0, 0)
 
     gate_part(c, lambda w: nown[c * per_core + w])
@@ -607,6 +623,7 @@
 
     @pl.when(inside[1])
     def _():
+        pl.semaphore_wait(ready_sem, 2)
         relay_own(1, 0)
 
     for step in range(1, cols_n):
@@ -794,7 +811,7 @@
             col_chunk(q - lag)
         return 0
 
-    lag = 2
+    lag = 3
     lax.fori_loop(0, chunks + lag, one_chunk, 0)
 
     for group, (first, chips) in enumerate(groups):
@@ -880,7 +897,7 @@
         functools.partial(grouped_kernel, states, rows_n, cols_n, chunks, per_core),
         in_specs=[pl.BlockSpec(memory_space=pl.ANY)] * 8,
         out_specs=pl.BlockSpec(memory_space=pltpu.VMEM),
-        out_shape=jax.ShapeDtypeStruct((columns, height, width_out), bf16),
+        out_shape=pltpu.VMEM((columns, height, width_out), bf16),
         scratch_shapes=[
             pltpu.VMEM((1, width), f32),
             pltpu.VMEM(w_in.shape, bf16),
@@ -916,7 +933,7 @@
             dma((local_chunks * lines,)), dma((chunks,)), dma((chunks,)), dma((chunks, 2)),
             dma((cols_n,)), dma((cols_n,)),
             dma((chunks, 2, 2 * lines)), dma((chunks,)), dma((chunks,)),
-            dma((cols_n, local_chunks)), dma((8,)),
+            dma((cols_n, local_chunks)), dma((9,)), pltpu.SemaphoreType.REGULAR,
         ],
         compiler_params=pltpu.CompilerParams(
             vmem_limit_bytes=VMEM_LIMIT, collective_id=0, has_side_effects=True

time: 47 us -> 42.8 us (0.911)
  Pallas kernels: 44.6 us -> 41.5 us
  local copies, waits for them, and re-layouts: 2.24 us -> 1.2 us
    pallas_call x1, Pallas kernels: 44.6 us -> 41.5 us  [per_device_grouped(): pl.pallas_call(functools.partial(grouped_kernel, states, rows_n, cols_n,...]
    transpose x1, local copies, waits for them, and re-layouts: 2.24 us -> 1.2 us  [per_device_grouped(): return out.transpose(1, 0, 2)]
where the time goes in v4:
time: 42.8 us; the launch traced here: 42.7 us
  Pallas kernels  41.5 us (97%)
  local copies, waits for them, and re-layouts  1.2 us (3%)
    pallas_call x1, Pallas kernels, per_device_grouped(): pl.pallas_call(functools.partial(grouped_kernel, states, rows_n, cols_n,...  41.5 us
    transpose x1, local copies, waits for them, and re-layouts, per_device_grouped(): return out.transpose(1, 0, 2)  1.2 us

profile of v4, /device:TPU:17, one launch (start us, length us, event | category | flops | bytes accessed | tf_op | source)
XLA Modules:
  0.0 42.7 jit_solution(7733363140284410637)
XLA Ops:
  0.0 41.5 %layer.1 = bf16[4,128,512]{2,1,0:T(8,128)(2,1)S(1)} custom-call(bf16[128,4,512]{2,1,0:T(4,128)(2,1)} %tok_ref.1, f32[1,512]{1,0:T(1,128)} %bitcast.7, bf16[512,2048]{1,0:T(8,128)(2,1)} %win_in.1, bf16[64,512]{1,0:T(8,128)(2,1)} %bitcast.5, f32[16,1024]{1,0:T(8,128)} %rrate_in.1, f32[16,1024]{1,0:T(8,128)} %crate_in.1, f32[4,1,256]{2,1,0:T(1,128)} %bitcast.6, ...), custom_call_target="tpu_custom_call" | custom-call | tf_op jit(solution)/shard_map/layer/pallas_call | solution.py:896
  41.5 1.2 %copy.9 = bf16[128,4,512]{2,1,0:T(4,128)(2,1)} copy(bf16[128,4,512]{2,0,1:T(8,128)(2,1)S(1)} %bitcast.4) | data formatting | bytes 1048576 | tf_op jit(solution)/shard_map/transpose | solution.py:946

commit v5 on v4

--- a/solution.py
+++ b/solution.py
@@ -397,7 +397,7 @@
     out_ref,
     gain_ref, win_ref, wbc_ref, rrate_ref, crate_ref, skip_ref, wout_ref,
     tokv, nown, ncol, tin_a, tin_b, tin_c, table, order_ref, u_ref, b_ref, c_ref, lag_ref,
-    rsend, rrecv, vcol, inject_ref, spread_ref, read_ref, hist, z_ref, gated_ref, stage, land, state_ref,
+    rsend, rrecv, vcol, inject_ref, spread_ref, read_ref, hist, z_ref, gated_ref, stage, state_ref,
     own_send_sem, own_sem, early_sem, relay_sem, csend_sem, crecv_sem, rsend_sem, rrecv_sem,
     osend_sem, orecv_sem, fetch_sem, ready_sem,
 ):
@@ -412,7 +412,7 @@
     lines = quarter * cols_n
     rows = chunk_rows // lines
     run = LANE_PAIR // states
-    parts = rsend_sem.shape[1]
+    parts = 2 if pairs % 2 == 0 else 1
     share = inner // parts
     r, c = lax.axis_index("rows"), lax.axis_index("cols")
 
@@ -422,33 +422,15 @@
     early = (0, quarter, 2 * quarter)
     line = r % quarter * cols_n + c
 
+    def half_of(q):
+        return (q + 1) % 2
+
     def chip_of(group, q, p):
         chip = groups[group][0] + p // cols_n
-        return chip + q % 2 * quarter if group == 2 else chip
+        return chip + half_of(q) * quarter if group == 2 else chip
 
     def slot(group, q):
         return q // 2 if group == 2 else q
-
-    barrier = pltpu.get_barrier_semaphore()
-
-    def greet(chip, core):
-        pl.semaphore_signal(barrier, inc=1, device_id={"rows": chip, "cols": core}, device_id_type=MESH)
-
-    for group, (first, chips) in enumerate(groups):
-        @pl.when(inside[group])
-        def _():
-            me = (r - first) * cols_n + c
-
-            def one(k, _):
-                @pl.when(k != me)
-                def _():
-                    greet(first + k // cols_n, k % cols_n)
-                return 0
-
-            lax.fori_loop(0, chips * cols_n, one, 0)
-            if group < 2:
-                for k in range(group + 1):
-                    greet(r + (k + 1) * quarter, c)
 
     head, rest = pl.ds(0, chunk_rows), pl.ds(chunk_rows, height - chunk_rows)
     fetches = [
@@ -462,6 +444,27 @@
     for fetch in fetches:
         fetch.start()
 
+    barrier = pltpu.get_barrier_semaphore()
+
+    def greet(chip, core):
+        pl.semaphore_signal(barrier, inc=1, device_id={"rows": chip, "cols": core}, device_id_type=MESH)
+
+    for group, (first, chips) in enumerate(groups):
+        @pl.when(inside[group])
+        def _():
+            me = (r - first) * cols_n + c
+
+            def one(k, _):
+                @pl.when(k != me)
+                def _():
+                    greet(first + k // cols_n, k % cols_n)
+                return 0
+
+            lax.fori_loop(0, chips * cols_n, one, 0)
+            if group < 2:
+                for k in range(group + 1):
+                    greet(r + (k + 1) * quarter, c)
+
     def normalise_part(part):
         first = part * chunk_rows
         flat = normalise(tokv[first : first + chunk_rows].astype(jnp.float32).reshape(-1, width), gain_ref[...])
@@ -493,7 +496,7 @@
         src = nown.at[:, pl.ds(pl.multiple_of(part * chunk_rows + p * rows, rows), rows)]
         dst = tins[group].at[slot(group, q), early[group] + r - groups[group][0]]
         remote = pltpu.make_async_remote_copy(
-            src_ref=src, dst_ref=dst, send_sem=own_send_sem.at[n], recv_sem=own_sem.at[q],
+            src_ref=src, dst_ref=dst, send_sem=own_send_sem.at[0], recv_sem=own_sem.at[q],
             device_id={"rows": chip, "cols": core}, device_id_type=MESH,
         )
         away = (chip != r) | (core != c)
@@ -536,6 +539,11 @@
     for step in range(1, cols_n):
         column_copy(step).start()
 
+    def drain_own(group):
+        count = local_chunks * (lines - 1) if group < 2 else local_chunks * lines - local_chunks // 2
+        sent = nown.at[:, pl.ds(0, count * rows)]
+        pltpu.make_async_copy(sent, sent, own_send_sem.at[0]).wait()
+
     def own_wait(group, q):
         part = tins[group].at[slot(group, q), pl.ds(early[group], groups[group][1])]
         pltpu.make_async_copy(part, part, own_sem.at[q]).wait()
@@ -550,7 +558,7 @@
         else:
             src = tin_b.at[q, pl.ds(which * quarter, quarter)]
             dst = tin_c.at[q // 2, pl.ds(which * quarter, quarter)]
-            chip = r + quarter + q % 2 * quarter
+            chip = r + quarter + half_of(q) * quarter
         return pltpu.make_async_remote_copy(
             src_ref=src, dst_ref=dst, send_sem=relay_sem.at[q, which], recv_sem=early_sem.at[q],
             device_id={"rows": chip}, device_id_type=MESH,
@@ -602,6 +610,7 @@
         spread_ref[i * states : (i + 1) * states] = wbc_ref[3 * states : 4 * states]
     crate_ref[...] = jnp.exp(-crate_ref[...])
     state_ref[...] = jnp.zeros(state_ref.shape, jnp.float32)
+    gated_ref[...] = jnp.zeros(gated_ref.shape, jnp.bfloat16)
     @pl.when(c == 0)
     def _():
         send_own(1, 2)
@@ -645,8 +654,8 @@
 
     @pl.when(inside[1])
     def _():
+        relay_own(1, 1)
         relay_early(1, 0)
-        relay_own(1, 1)
 
     def result_copy(group, q, part, k):
         first, chips = groups[group]
@@ -654,7 +663,7 @@
         some = pl.ds(pl.multiple_of(part * share, share), share)
         src, dst = rsend.at[slot(group, q), g, :, :, some], rrecv.at[q, line, :, :, some]
         remote = pltpu.make_async_remote_copy(
-            src_ref=src, dst_ref=dst, send_sem=rsend_sem.at[slot(group, q), part, k], recv_sem=rrecv_sem.at[q],
+            src_ref=src, dst_ref=dst, send_sem=rsend_sem.at[slot(group, q)], recv_sem=rrecv_sem.at[q],
             device_id={"rows": first + g // cols_n, "cols": g % cols_n}, device_id_type=MESH,
         )
         return remote, lambda: pltpu.make_async_copy(src, dst, rrecv_sem.at[q])
@@ -719,9 +728,13 @@
 
         lax.fori_loop(0, parts, one_part, 0)
 
+    def out_part(core, i):
+        first = pl.multiple_of(i * chunk_rows, chunk_rows)
+        return out_ref.at[pl.ds(core * per_core, per_core), pl.ds(first, chunk_rows)]
+
     def out_copy(q):
         return pltpu.make_async_remote_copy(
-            src_ref=stage.at[q], dst_ref=land.at[c, q % local_chunks],
+            src_ref=stage.at[q], dst_ref=out_part(c, q % local_chunks),
             send_sem=osend_sem.at[q], recv_sem=orecv_sem.at[c, q % local_chunks],
             device_id={"cols": q // local_chunks}, device_id_type=MESH,
         )
@@ -735,6 +748,7 @@
                     vcol[t, w * chunk_rows + p * rows : w * chunk_rows + (p + 1) * rows] = (
                         value[:, t * LANES : (t + 1) * LANES]
                     )
+        project((q + chunks - 1) % chunks)
         halves = range(0, states, SUBLANES)
 
         def one_run(i):
@@ -765,29 +779,37 @@
                         )
                     gate = z_ref[pl.ds(patch, run), t * LANES : (t + 1) * LANES].astype(jnp.float32)
                     both = mixed[:, t % 2 * LANES : (t % 2 + 1) * LANES] + vcol[t, pl.ds(here, run), :]
-                    gated_ref[pl.ds(here, run), t * LANES : (t + 1) * LANES] = (
+                    gated_ref[q % 2, pl.ds(here, run), t * LANES : (t + 1) * LANES] = (
                         both * (gate / (1.0 + jnp.exp(-gate)))
                     ).astype(jnp.bfloat16)
 
         for i in range(chunk_rows // run):
             one_run(i)
-        result = jnp.dot(gated_ref[...], wout_ref[...], preferred_element_type=jnp.float32).astype(jnp.bfloat16)
+
+        @pl.when(q > 0)
+        def _():
+            send_out(q - 1)
+
+    def project(q):
+        result = jnp.dot(gated_ref[q % 2], wout_ref[...], preferred_element_type=jnp.float32).astype(jnp.bfloat16)
+        stage[q] = result.reshape(per_core, chunk_rows, -1)
+
+    def send_out(q):
         home = q // local_chunks
 
         @pl.when(home == c)
         def _():
-            land[c, q % local_chunks] = result
+            pltpu.make_async_copy(stage.at[q], out_part(c, q % local_chunks), orecv_sem.at[c, q % local_chunks]).start()
 
         @pl.when(home != c)
         def _():
-            stage[q] = result
             out_copy(q).start()
 
     def one_chunk(q, _):
         for group in range(3):
             mine = inside[group] & (q < chunks)
             if group == 2:
-                mine = mine & (q % 2 == (r - 2 * quarter) // quarter)
+                mine = mine & (half_of(q) == (r - 2 * quarter) // quarter)
 
             @pl.when(mine)
             def _():
@@ -811,42 +833,33 @@
             col_chunk(q - lag)
         return 0
 
+    @pl.when(inside[2])
+    def _():
+        drain_own(2)
+
     lag = 3
     lax.fori_loop(0, chunks + lag, one_chunk, 0)
+    project(chunks - 1)
+    send_out(chunks - 1)
 
     for group, (first, chips) in enumerate(groups):
         @pl.when(inside[group])
         def _():
-            def drain_tokens(n, _):
-                away, remote, _ = token_copy(group, n)
-
-                @pl.when(away)
-                def _():
-                    remote.wait_send()
-                return 0
-
-            lax.fori_loop(0, local_chunks * lines, drain_tokens, 0)
+            if group < 2:
+                drain_own(group)
 
             def drain_chunk(q, _):
                 if group < 2:
                     relay_copy(group, q, 1).wait_send()
                 if group == 1:
                     relay_copy(group, q, 0).wait_send()
-
-                def one(k, _):
-                    for part in range(parts):
-                        result_copy(group, q, part, k)[0].wait_send()
-                    return 0
-
-                if group == 2:
-                    @pl.when(q % 2 == (r - 2 * quarter) // quarter)
-                    def _():
-                        lax.fori_loop(1, chips * cols_n, one, 0)
-                else:
-                    lax.fori_loop(1, chips * cols_n, one, 0)
                 return 0
 
-            lax.fori_loop(0, chunks, drain_chunk, 0)
+            if group < 2:
+                lax.fori_loop(0, chunks, drain_chunk, 0)
+            for at in range(chunks // (1 + group // 2)):
+                sent = rsend.at[at, pl.ds(0, chips * cols_n - 1)]
+                pltpu.make_async_copy(sent, sent, rsend_sem.at[at]).wait()
 
     for step in range(1, cols_n):
         column_copy(step).wait_send()
@@ -859,18 +872,9 @@
 
     lax.fori_loop(0, chunks, drain_out, 0)
     for source in range(cols_n):
-        @pl.when(source != c)
-        def _():
-            for i in range(local_chunks):
-                pltpu.make_async_copy(
-                    land.at[source, i], land.at[source, i], orecv_sem.at[source, i]
-                ).wait()
-    for source in range(cols_n):
         for i in range(local_chunks):
-            for w in range(per_core):
-                out_ref[source * per_core + w, i * chunk_rows : (i + 1) * chunk_rows] = (
-                    land[source, i, w * chunk_rows : (w + 1) * chunk_rows]
-                )
+            part = out_part(source, i)
+            pltpu.make_async_copy(part, part, orecv_sem.at[source, i]).wait()
 
 
 def per_device_grouped(chunks, tokens, norm_gain, w_in, w_bc, rate_row, rate_col, skip_gain, w_out):
@@ -896,7 +900,7 @@
     out = pl.pallas_call(
         functools.partial(grouped_kernel, states, rows_n, cols_n, chunks, per_core),
         in_specs=[pl.BlockSpec(memory_space=pl.ANY)] * 8,
-        out_specs=pl.BlockSpec(memory_space=pltpu.VMEM),
+        out_specs=pl.BlockSpec(memory_space=pl.ANY),
         out_shape=pltpu.VMEM((columns, height, width_out), bf16),
         scratch_shapes=[
             pltpu.VMEM((1, width), f32),
@@ -926,13 +930,12 @@
             pltpu.VMEM((patches, LANE_PAIR), bf16),
             pltpu.VMEM((per_core * chunk_rows * states // LANE_PAIR, tiles, LANE_PAIR, LANES), bf16),
             pltpu.VMEM((patches, inner), bf16),
-            pltpu.VMEM((per_core * chunk_rows, inner), bf16),
-            pltpu.VMEM((chunks, per_core * chunk_rows, width_out), bf16),
-            pltpu.VMEM((cols_n, local_chunks, per_core * chunk_rows, width_out), bf16),
+            pltpu.VMEM((2, per_core * chunk_rows, inner), bf16),
+            pltpu.VMEM((chunks, per_core, chunk_rows, width_out), bf16),
             pltpu.VMEM((per_core, states, inner), f32),
-            dma((local_chunks * lines,)), dma((chunks,)), dma((chunks,)), dma((chunks, 2)),
+            dma((1,)), dma((chunks,)), dma((chunks,)), dma((chunks, 2)),
             dma((cols_n,)), dma((cols_n,)),
-            dma((chunks, 2, 2 * lines)), dma((chunks,)), dma((chunks,)),
+            dma((chunks,)), dma((chunks,)), dma((chunks,)),
             dma((cols_n, local_chunks)), dma((9,)), pltpu.SemaphoreType.REGULAR,
         ],
         compiler_params=pltpu.CompilerParams(

time: 42.8 us -> 40.4 us (0.944)
  Pallas kernels: 41.5 us -> 39 us
    pallas_call x1, Pallas kernels: 41.5 us -> 39 us  [per_device_grouped(): pl.pallas_call(functools.partial(grouped_kernel, states, rows_n, cols_n,...]
where the time goes in v5:
time: 40.4 us; the launch traced here: 40.2 us
  Pallas kernels  39 us (97%)
  local copies, waits for them, and re-layouts  1.2 us (3%)
    pallas_call x1, Pallas kernels, per_device_grouped(): pl.pallas_call(functools.partial(grouped_kernel, states, rows_n, cols_n,...  39 us
    transpose x1, local copies, waits for them, and re-layouts, per_device_grouped(): return out.transpose(1, 0, 2)  1.2 us

profile of v5, /device:TPU:17, one launch (start us, length us, event | category | flops | bytes accessed | tf_op | source)
XLA Modules:
  0.0 40.2 jit_solution(16750478790492261587)
XLA Ops:
  0.0 39.0 %layer.1 = bf16[4,128,512]{2,1,0:T(8,128)(2,1)S(1)} custom-call(bf16[128,4,512]{2,1,0:T(4,128)(2,1)} %tok_ref.1, f32[1,512]{1,0:T(1,128)} %bitcast.7, bf16[512,2048]{1,0:T(8,128)(2,1)} %win_in.1, bf16[64,512]{1,0:T(8,128)(2,1)} %bitcast.5, f32[16,1024]{1,0:T(8,128)} %rrate_in.1, f32[16,1024]{1,0:T(8,128)} %crate_in.1, f32[4,1,256]{2,1,0:T(1,128)} %bitcast.6, ...), custom_call_target="tpu_custom_call" | custom-call | tf_op jit(solution)/shard_map/layer/pallas_call | solution.py:900
  39.0 1.2 %copy.9 = bf16[128,4,512]{2,1,0:T(4,128)(2,1)} copy(bf16[128,4,512]{2,0,1:T(8,128)(2,1)S(1)} %bitcast.4) | data formatting | bytes 1048576 | tf_op jit(solution)/shard_map/transpose | solution.py:949

commit v6 on v5

--- a/solution.py
+++ b/solution.py
@@ -396,9 +396,9 @@
     tok_ref, gain_in, win_in, wbc_in, rrate_in, crate_in, skip_in, wout_in,
     out_ref,
     gain_ref, win_ref, wbc_ref, rrate_ref, crate_ref, skip_ref, wout_ref,
-    tokv, nown, ncol, tin_a, tin_b, tin_c, table, order_ref, u_ref, b_ref, c_ref, lag_ref,
+    tokv, nown, ncol, tin_a, tin_b, tin_c, table, order_ref, u_ref, b_ref, uown_ref, bown_ref, cown_ref, lag_ref,
     rsend, rrecv, vcol, inject_ref, spread_ref, read_ref, hist, z_ref, gated_ref, stage, state_ref,
-    own_send_sem, own_sem, early_sem, relay_sem, csend_sem, crecv_sem, rsend_sem, rrecv_sem,
+    own_send_sem, next_send_sem, own_sem, early_sem, relay_sem, csend_sem, crecv_sem, rsend_sem, rrecv_sem,
     osend_sem, orecv_sem, fetch_sem, ready_sem,
 ):
     height, columns, width = tok_ref.shape
@@ -412,7 +412,7 @@
     lines = quarter * cols_n
     rows = chunk_rows // lines
     run = LANE_PAIR // states
-    parts = 2 if pairs % 2 == 0 else 1
+    parts = 1
     share = inner // parts
     r, c = lax.axis_index("rows"), lax.axis_index("cols")
 
@@ -461,9 +461,15 @@
                 return 0
 
             lax.fori_loop(0, chips * cols_n, one, 0)
-            if group < 2:
-                for k in range(group + 1):
+            if group == 1:
+                for k in range(2):
                     greet(r + (k + 1) * quarter, c)
+
+                def back(k, _):
+                    greet(k // cols_n, k % cols_n)
+                    return 0
+
+                lax.fori_loop(0, lines, back, 0)
 
     def normalise_part(part):
         first = part * chunk_rows
@@ -483,8 +489,8 @@
     for group, (first, chips) in enumerate(groups):
         @pl.when(inside[group])
         def _():
-            pl.semaphore_wait(barrier, chips * cols_n - 1 + (group > 0))
-            if group:
+            pl.semaphore_wait(barrier, chips * cols_n - 1 + (lines, 0, 1)[group])
+            if group == 2:
                 pl.semaphore_signal(
                     ready_sem, inc=1, device_id={"rows": first - quarter + (r - first) % quarter}, device_id_type=MESH
                 )
@@ -520,10 +526,29 @@
 
                 lax.fori_loop(low * lines, high * lines, one, 0)
 
-    @pl.when(c == 0)
-    def _():
-        send_own(0, 1)
-
+    def next_copy(part, p):
+        p = (p + line) % lines
+        return pltpu.make_async_remote_copy(
+            src_ref=nown.at[:, pl.ds(pl.multiple_of(part * chunk_rows + p * rows, rows), rows)],
+            dst_ref=tin_b.at[part, r], send_sem=next_send_sem.at[0], recv_sem=early_sem.at[part],
+            device_id={"rows": quarter + p // cols_n, "cols": p % cols_n}, device_id_type=MESH,
+        )
+
+    def send_first(part):
+        @pl.when(c == 0)
+        def _():
+            send_own(part, part + 1)
+
+        @pl.when(inside[0] & (c == 0))
+        def _():
+            def one(p, _):
+                next_copy(part, p).start()
+                return 0
+
+            lax.fori_loop(0, lines, one, 0)
+
+    direct = 2
+    send_first(0)
     fetches[2].wait()
     for part in range(1, local_chunks):
         normalise_part(part)
@@ -611,24 +636,12 @@
     crate_ref[...] = jnp.exp(-crate_ref[...])
     state_ref[...] = jnp.zeros(state_ref.shape, jnp.float32)
     gated_ref[...] = jnp.zeros(gated_ref.shape, jnp.bfloat16)
+    send_first(1)
+    gate_part(c, lambda w: nown[c * per_core + w])
+
     @pl.when(c == 0)
     def _():
-        send_own(1, 2)
-
-    @pl.when(inside[0])
-    def _():
-        pl.semaphore_wait(ready_sem, 1)
-        relay_own(0, 0)
-
-    gate_part(c, lambda w: nown[c * per_core + w])
-
-    @pl.when(c == 0)
-    def _():
-        send_own(2, local_chunks)
-
-    @pl.when(inside[0])
-    def _():
-        relay_own(0, 1)
+        send_own(direct, local_chunks)
 
     @pl.when(inside[1])
     def _():
@@ -650,12 +663,14 @@
             relay_own(0, q)
             return 0
 
-        lax.fori_loop(2, local_chunks, one, 0)
+        for q in range(direct):
+            own_wait(0, q)
+        lax.fori_loop(direct, local_chunks, one, 0)
 
     @pl.when(inside[1])
     def _():
+        relay_early(1, 0)
         relay_own(1, 1)
-        relay_early(1, 0)
 
     def result_copy(group, q, part, k):
         first, chips = groups[group]
@@ -668,25 +683,50 @@
         )
         return remote, lambda: pltpu.make_async_copy(src, dst, rrecv_sem.at[q])
 
+    def rounded(value):
+        return value.astype(jnp.bfloat16).astype(jnp.float32)
+
+    def project_in(normed, k):
+        return rounded(jnp.dot(
+            normed, win_ref[:, k * LANE_PAIR : (k + 1) * LANE_PAIR], preferred_element_type=jnp.float32
+        ))
+
+    def own_part(group, q):
+        chips = groups[group][1]
+        before = early[group]
+        count = chips * columns * rows
+        ready = slot(group, q) if group == 2 else 0
+        if group == 2:
+            own_wait(group, q)
+        normed = tins[group][slot(group, q), before : before + chips].reshape(count, width)
+        bown_ref[ready, :count] = rounded(transposed_dot(normed, wbc_ref[:states]))
+        cown_ref[ready, :count] = rounded(transposed_dot(normed, wbc_ref[states : 2 * states]))
+        for k in range(pairs):
+            uown_ref[ready, k, :count] = project_in(normed, k)
+
     def row_chunk(group, q):
         chips = groups[group][1]
         before = early[group]
         at = slot(group, q)
         tin = tins[group]
-        if group == 2:
-            early_wait(group, q)
-            own_wait(group, q)
         out_cols, pre_cols = chips * columns, before * columns
         all_cols = out_cols + pre_cols
-        normed = tin[at].reshape(all_cols * rows, width)
-        b_ref[: all_cols * rows] = transposed_dot(normed, wbc_ref[:states]).astype(jnp.bfloat16).astype(jnp.float32)
-        c_ref[: out_cols * rows] = transposed_dot(
-            normed[pre_cols * rows :], wbc_ref[states : 2 * states]
-        ).astype(jnp.bfloat16).astype(jnp.float32)
-        for k in range(pairs):
-            u_ref[k, : all_cols * rows] = jnp.dot(
-                normed, win_ref[:, k * LANE_PAIR : (k + 1) * LANE_PAIR], preferred_element_type=jnp.float32
-            ).astype(jnp.bfloat16).astype(jnp.float32)
+        if group < 2:
+            own_part(group, q)
+        else:
+            early_wait(group, q)
+        ready = at if group == 2 else 0
+        if before:
+            normed = tin[at, :before].reshape(pre_cols * rows, width)
+            b_ref[: pre_cols * rows] = rounded(transposed_dot(normed, wbc_ref[:states]))
+            for k in range(pairs):
+                u_ref[k, : pre_cols * rows] = project_in(normed, k)
+        b_ref[pre_cols * rows : all_cols * rows] = bown_ref[ready, : out_cols * rows]
+
+        def value_of(k, col):
+            if col < pre_cols:
+                return u_ref[k, col * rows : (col + 1) * rows]
+            return uown_ref[ready, k, (col - pre_cols) * rows : (col - pre_cols + 1) * rows]
 
         def span(d):
             low = max(0, d - pre_cols)
@@ -695,21 +735,19 @@
         for d in range(all_cols):
             low, count, source = span(d)
             lag_ref[d, : count * rows] = (
-                c_ref[low * rows : out_cols * rows] * b_ref[source * rows : (source + count) * rows]
+                cown_ref[ready, low * rows : out_cols * rows] * b_ref[source * rows : (source + count) * rows]
             ).astype(jnp.bfloat16)
 
         def one_pair(k):
             skip = skip_ref[k]
             sums = [
-                skip * u_ref[k, (pre_cols + o) * rows : (pre_cols + o + 1) * rows] for o in range(out_cols)
+                skip * value_of(k, pre_cols + o) for o in range(out_cols)
             ]
             for d in range(all_cols):
                 low, count, source = span(d)
                 weight = jnp.dot(lag_ref[d, : count * rows], table[k, d], preferred_element_type=jnp.float32)
                 for i in range(count):
-                    sums[low + i] += weight[i * rows : (i + 1) * rows] * u_ref[
-                        k, (source + i) * rows : (source + i + 1) * rows
-                    ]
+                    sums[low + i] += weight[i * rows : (i + 1) * rows] * value_of(k, source + i)
             some = pl.ds(pl.multiple_of(k * LANE_PAIR, LANE_PAIR), LANE_PAIR)
             for o in range(out_cols):
                 rsend[at, o // per_core, o % per_core, :, some] = sums[o].astype(jnp.bfloat16)
@@ -814,6 +852,10 @@
             @pl.when(mine)
             def _():
                 row_chunk(group, q)
+                if group == 2:
+                    @pl.when(q + 2 < chunks)
+                    def _():
+                        own_part(group, q + 2)
 
             if group == 0:
                 @pl.when(inside[group] & (q + local_chunks < chunks))
@@ -835,7 +877,7 @@
 
     @pl.when(inside[2])
     def _():
-        drain_own(2)
+        own_part(2, 1 - (r - 2 * quarter) // quarter)
 
     lag = 3
     lax.fori_loop(0, chunks + lag, one_chunk, 0)
@@ -845,18 +887,21 @@
     for group, (first, chips) in enumerate(groups):
         @pl.when(inside[group])
         def _():
-            if group < 2:
-                drain_own(group)
+            drain_own(group)
 
             def drain_chunk(q, _):
-                if group < 2:
-                    relay_copy(group, q, 1).wait_send()
+                relay_copy(group, q, 1).wait_send()
                 if group == 1:
                     relay_copy(group, q, 0).wait_send()
                 return 0
 
+            if group == 0:
+                @pl.when(c == 0)
+                def _():
+                    sent = nown.at[:, pl.ds(0, direct * lines * rows)]
+                    pltpu.make_async_copy(sent, sent, next_send_sem.at[0]).wait()
             if group < 2:
-                lax.fori_loop(0, chunks, drain_chunk, 0)
+                lax.fori_loop((direct, 0)[group], chunks, drain_chunk, 0)
             for at in range(chunks // (1 + group // 2)):
                 sent = rsend.at[at, pl.ds(0, chips * cols_n - 1)]
                 pltpu.make_async_copy(sent, sent, rsend_sem.at[at]).wait()
@@ -920,7 +965,9 @@
             pltpu.VMEM((width // LANES, height * columns, LANES), f32),
             pltpu.VMEM((pairs, held, LANE_PAIR), f32),
             pltpu.VMEM((held, states), f32),
-            pltpu.VMEM((outs, states), f32),
+            pltpu.VMEM((chunks // 2, pairs, outs, LANE_PAIR), f32),
+            pltpu.VMEM((chunks // 2, outs, states), f32),
+            pltpu.VMEM((chunks // 2, outs, states), f32),
             pltpu.VMEM((lags, outs, states), bf16),
             pltpu.VMEM((chunks, 2 * lines, per_core, rows, inner), bf16),
             pltpu.VMEM((chunks, lines, per_core, rows, inner), bf16),
@@ -933,7 +980,7 @@
             pltpu.VMEM((2, per_core * chunk_rows, inner), bf16),
             pltpu.VMEM((chunks, per_core, chunk_rows, width_out), bf16),
             pltpu.VMEM((per_core, states, inner), f32),
-            dma((1,)), dma((chunks,)), dma((chunks,)), dma((chunks, 2)),
+            dma((1,)), dma((1,)), dma((chunks,)), dma((chunks,)), dma((chunks, 2)),
             dma((cols_n,)), dma((cols_n,)),
             dma((chunks,)), dma((chunks,)), dma((chunks,)),
             dma((cols_n, local_chunks)), dma((9,)), pltpu.SemaphoreType.REGULAR,

time: 40.4 us -> 39.9 us (0.988); the launches traced: 40.2 us -> 39.2 us
  Pallas kernels: 39 us -> 38 us
    pallas_call x1, Pallas kernels: 39 us -> 38 us  [per_device_grouped(): pl.pallas_call(functools.partial(grouped_kernel, states, rows_n, cols_n,...]
where the time goes in v6:
time: 39.9 us; the launch traced here: 39.2 us
  Pallas kernels  38 us (95%)
  local copies, waits for them, and re-layouts  1.2 us (3%)
    pallas_call x1, Pallas kernels, per_device_grouped(): pl.pallas_call(functools.partial(grouped_kernel, states, rows_n, cols_n,...  38 us
    transpose x1, local copies, waits for them, and re-layouts, per_device_grouped(): return out.transpose(1, 0, 2)  1.2 us

profile of v6, /device:TPU:17, one launch (start us, length us, event | category | flops | bytes accessed | tf_op | source)
XLA Modules:
  0.0 39.2 jit_solution(1409718697945158482)
XLA Ops:
  0.0 38.0 %layer.1 = bf16[4,128,512]{2,1,0:T(8,128)(2,1)S(1)} custom-call(bf16[128,4,512]{2,1,0:T(4,128)(2,1)} %tok_ref.1, f32[1,512]{1,0:T(1,128)} %bitcast.7, bf16[512,2048]{1,0:T(8,128)(2,1)} %win_in.1, bf16[64,512]{1,0:T(8,128)(2,1)} %bitcast.5, f32[16,1024]{1,0:T(8,128)} %rrate_in.1, f32[16,1024]{1,0:T(8,128)} %crate_in.1, f32[4,1,256]{2,1,0:T(1,128)} %bitcast.6, ...), custom_call_target="tpu_custom_call" | custom-call | tf_op jit(solution)/shard_map/layer/pallas_call | solution.py:945
  38.0 1.2 %copy.9 = bf16[128,4,512]{2,1,0:T(4,128)(2,1)} copy(bf16[128,4,512]{2,0,1:T(8,128)(2,1)S(1)} %bitcast.4) | data formatting | bytes 1048576 | tf_op jit(solution)/shard_map/transpose | solution.py:996

commit v7 on v6

--- a/solution.py
+++ b/solution.py
@@ -732,18 +732,22 @@
             low = max(0, d - pre_cols)
             return low, out_cols - low, pre_cols + low - d
 
-        for d in range(all_cols):
+        for d in range(1, all_cols):
             low, count, source = span(d)
             lag_ref[d, : count * rows] = (
                 cown_ref[ready, low * rows : out_cols * rows] * b_ref[source * rows : (source + count) * rows]
             ).astype(jnp.bfloat16)
 
+        here = jnp.sum(
+            cown_ref[ready, : out_cols * rows] * b_ref[pre_cols * rows : all_cols * rows], axis=1, keepdims=True
+        )
+
         def one_pair(k):
             skip = skip_ref[k]
             sums = [
-                skip * value_of(k, pre_cols + o) for o in range(out_cols)
+                (skip + here[o * rows : (o + 1) * rows]) * value_of(k, pre_cols + o) for o in range(out_cols)
             ]
-            for d in range(all_cols):
+            for d in range(1, all_cols):
                 low, count, source = span(d)
                 weight = jnp.dot(lag_ref[d, : count * rows], table[k, d], preferred_element_type=jnp.float32)
                 for i in range(count):

time: 39.9 us -> 39.8 us (level)
  no operation moved by 1% of the time
where the time goes in v7:
time: 39.8 us; the launch traced here: 39.2 us
  Pallas kernels  38 us (95%)
  local copies, waits for them, and re-layouts  1.2 us (3%)
    pallas_call x1, Pallas kernels, per_device_grouped(): pl.pallas_call(functools.partial(grouped_kernel, states, rows_n, cols_n,...  38 us
    transpose x1, local copies, waits for them, and re-layouts, per_device_grouped(): return out.transpose(1, 0, 2)  1.2 us

profile of v7, /device:TPU:17, one launch (start us, length us, event | category | flops | bytes accessed | tf_op | source)
XLA Modules:
  0.0 39.2 jit_solution(948062955984715718)
XLA Ops:
  0.0 38.0 %layer.1 = bf16[4,128,512]{2,1,0:T(8,128)(2,1)S(1)} custom-call(bf16[128,4,512]{2,1,0:T(4,128)(2,1)} %tok_ref.1, f32[1,512]{1,0:T(1,128)} %bitcast.7, bf16[512,2048]{1,0:T(8,128)(2,1)} %win_in.1, bf16[64,512]{1,0:T(8,128)(2,1)} %bitcast.5, f32[16,1024]{1,0:T(8,128)} %rrate_in.1, f32[16,1024]{1,0:T(8,128)} %crate_in.1, f32[4,1,256]{2,1,0:T(1,128)} %bitcast.6, ...), custom_call_target="tpu_custom_call" | custom-call | tf_op jit(solution)/shard_map/layer/pallas_call | solution.py:949
  38.0 1.2 %copy.9 = bf16[128,4,512]{2,1,0:T(4,128)(2,1)} copy(bf16[128,4,512]{2,0,1:T(8,128)(2,1)S(1)} %bitcast.4) | data formatting | bytes 1048576 | tf_op jit(solution)/shard_map/transpose | solution.py:1000

commit v8 on v7

--- a/solution.py
+++ b/solution.py
@@ -674,7 +674,9 @@
 
     def result_copy(group, q, part, k):
         first, chips = groups[group]
-        g = ((r - first) * cols_n + c + k) % (chips * cols_n)
+        count = chips * cols_n
+        k = jnp.where(k == 0, 0, (k + count // 2 - 2) % (count - 1) + 1)
+        g = ((r - first) * cols_n + c + k) % count
         some = pl.ds(pl.multiple_of(part * share, share), share)
         src, dst = rsend.at[slot(group, q), g, :, :, some], rrecv.at[q, line, :, :, some]
         remote = pltpu.make_async_remote_copy(
@@ -759,13 +761,13 @@
         def one_part(part, _):
             for k in range(pairs // parts):
                 one_pair(part * (pairs // parts) + k)
-            result_copy(group, q, part, 0)[1]().start()
 
             def send_result(k, _):
                 result_copy(group, q, part, k)[0].start()
                 return 0
 
             lax.fori_loop(1, chips * cols_n, send_result, 0)
+            result_copy(group, q, part, 0)[1]().start()
             return 0
 
         lax.fori_loop(0, parts, one_part, 0)

time: 39.8 us -> 39.7 us (level)
  no operation moved by 1% of the time
where the time goes in v8:
time: 39.7 us; the launch traced here: 39.2 us
  Pallas kernels  38 us (96%)
  local copies, waits for them, and re-layouts  1.2 us (3%)
    pallas_call x1, Pallas kernels, per_device_grouped(): pl.pallas_call(functools.partial(grouped_kernel, states, rows_n, cols_n,...  38 us
    transpose x1, local copies, waits for them, and re-layouts, per_device_grouped(): return out.transpose(1, 0, 2)  1.2 us

profile of v8, /device:TPU:17, one launch (start us, length us, event | category | flops | bytes accessed | tf_op | source)
XLA Modules:
  0.0 39.2 jit_solution(10894689131609836390)
XLA Ops:
  0.0 38.0 %layer.1 = bf16[4,128,512]{2,1,0:T(8,128)(2,1)S(1)} custom-call(bf16[128,4,512]{2,1,0:T(4,128)(2,1)} %tok_ref.1, f32[1,512]{1,0:T(1,128)} %bitcast.7, bf16[512,2048]{1,0:T(8,128)(2,1)} %win_in.1, bf16[64,512]{1,0:T(8,128)(2,1)} %bitcast.5, f32[16,1024]{1,0:T(8,128)} %rrate_in.1, f32[16,1024]{1,0:T(8,128)} %crate_in.1, f32[4,1,256]{2,1,0:T(1,128)} %bitcast.6, ...), custom_call_target="tpu_custom_call" | custom-call | tf_op jit(solution)/shard_map/layer/pallas_call | solution.py:951
  38.0 1.2 %copy.9 = bf16[128,4,512]{2,1,0:T(4,128)(2,1)} copy(bf16[128,4,512]{2,0,1:T(8,128)(2,1)S(1)} %bitcast.4) | data formatting | bytes 1048576 | tf_op jit(solution)/shard_map/transpose | solution.py:1002
